TPU v7x, 32 devices: a whole 2x2x4 slice. The times are simulated.
32 devices in a mesh: fsdp: 4 (over y, x), context: 4 (over z), tensor: 2 (over core).
Axes of the slice: x: 2, y: 2, z: 4, core: 2. Of those that a mesh axis runs over, the one named last changes fastest.
Arguments:
- inputs: bfloat16 [2048, 1024], P(('fsdp', 'context')), may hold values from -6 to 6
- seq_lengths: int32 [4, 2], P('fsdp'), may hold values from 170 to 342, as said below
- norm_gains: bfloat16 [2, 1024], P(None, ('fsdp', 'context')), may hold values from 0.5 to 1.5
- mamba_in: bfloat16 [1024, 2, 1536], P(('fsdp', 'context'), None, 'tensor'), may hold values from -0.1875 to 0.1875
- dt_proj: bfloat16 [1024, 24], P(('fsdp', 'context'), 'tensor'), may hold values from -0.1875 to 0.1875
- bc_proj: bfloat16 [1024, 256], P(('fsdp', 'context')), may hold values from -0.1875 to 0.1875
- mamba_chan: bfloat16 [24, 384], P('tensor', ('fsdp', 'context')), may hold values from -0.5 to 1.25
- bc_conv: bfloat16 [5, 256], P(None, ('fsdp', 'context')), may hold values from -0.5 to 0.5
- head_params: float32 [3, 24], P(None, 'tensor'), may hold values from -10 to 3, as said below
- query_proj: bfloat16 [1024, 512], P(('fsdp', 'context'), 'tensor'), may hold values from -0.1875 to 0.1875
- kv_proj: bfloat16 [1024, 2, 128], P(('fsdp', 'context'), None, 'tensor'), may hold values from -0.1875 to 0.1875
- attn_out: bfloat16 [512, 1024], P('tensor', ('fsdp', 'context')), may hold values from -3 to 3
- mamba_out: bfloat16 [1536, 1024], P('tensor', ('fsdp', 'context')), may hold values from -0.15625 to 0.15625
- mlp_in: bfloat16 [1024, 2, 2048], P(('fsdp', 'context'), None, 'tensor'), may hold values from -0.1875 to 0.1875
- mlp_out: bfloat16 [2048, 1024], P('tensor', ('fsdp', 'context')), may hold values from -0.125 to 0.125
- out_grad: bfloat16 [2048, 1024], P(('fsdp', 'context')), may hold values from -6 to 6
Outputs:
- output: bfloat16 [2048, 1024], P(('fsdp', 'context'))
- input_grad: float32 [2048, 1024], P(('fsdp', 'context'))
- grad_norm_gains: float32 [2, 1024], P(None, ('fsdp', 'context'))
- grad_mamba_in: float32 [1024, 2, 1536], P(('fsdp', 'context'), None, 'tensor')
- grad_dt_proj: float32 [1024, 24], P(('fsdp', 'context'), 'tensor')
- grad_bc_proj: float32 [1024, 256], P(('fsdp', 'context'))
- grad_mamba_chan: float32 [24, 384], P('tensor', ('fsdp', 'context'))
- grad_bc_conv: float32 [5, 256], P(None, ('fsdp', 'context'))
- grad_head_params: float32 [3, 24], P(None, 'tensor')
- grad_query_proj: float32 [1024, 512], P(('fsdp', 'context'), 'tensor')
- grad_kv_proj: float32 [1024, 2, 128], P(('fsdp', 'context'), None, 'tensor')
- grad_attn_out: float32 [512, 1024], P('tensor', ('fsdp', 'context'))
- grad_mamba_out: float32 [1536, 1024], P('tensor', ('fsdp', 'context'))
- grad_mlp_in: float32 [1024, 2, 2048], P(('fsdp', 'context'), None, 'tensor')
- grad_mlp_out: float32 [2048, 1024], P('tensor', ('fsdp', 'context'))
Inputs may be any that keep to these rules, and one draw needn't show every extreme that they name: `seq_lengths`: row g lists, in order, the lengths of the 2 sequences that fill the 512 rows of token group g; they sum to 512. `head_params`: rows are step bias, log decay rate and skip weight of a head.
All inputs are finite; a program needn't handle non-finite values.
Results may differ from a plain program's by a relative error of at most 0.018.
Values may be sent and summed in bfloat16 or wider, within the bound.
No kernel may reach another device: no remote copies, remote signals or barrier semaphores. Data moves between devices by JAX's collectives and lax.ppermute only.
A program may use at most 128 MiB of HBM per device.

v0:
```python
import jax
import jax.numpy as jnp
from jax import lax
from jax.experimental import pallas as pl
from jax.experimental.pallas import tpu as pltpu
from jax.sharding import PartitionSpec as P


HDIM = 64
NSTATE = 128
KCONV = 4
NORM_EPS = 1e-05
ROPE_BASE = 100000000000.0
EXACT = lax.Precision.HIGHEST
BF = jnp.bfloat16
F32 = jnp.float32


def swap_pair(block):
    return lax.ppermute(block, "tensor", [(0, 1), (1, 0)])


def join_pair(own, other, place, axis):
    low = jnp.where(place == 0, own, other)
    high = jnp.where(place == 0, other, own)
    return jnp.stack([low, high], axis=axis)


def exchange(blocks, axis):
    return lax.all_to_all(blocks, axis, 0, 0, tiled=True)


def spread(block, axis):
    return exchange(jnp.broadcast_to(block[None], (lax.axis_size(axis),) + block.shape), axis)


def hops(axis):
    count = lax.axis_size(axis)
    place = lax.axis_index(axis)
    for step in range(1, count):
        route = [(i, (i + step) % count) for i in range(count)]
        yield route, (place + step) % count, (place - step) % count


def spread_async(block, axis):
    count = lax.axis_size(axis)
    got = [(lax.ppermute(block, axis, route), source) for route, _, source in hops(axis)]
    if block.size > 1 << 18:
        whole = jnp.zeros((count,) + block.shape, block.dtype)
        whole = lax.dynamic_update_index_in_dim(whole, block, lax.axis_index(axis), 0)
        for piece, source in got:
            whole = lax.dynamic_update_index_in_dim(whole, piece, source, 0)
        return whole
    place = lax.axis_index(axis)
    pieces = [block] + [piece for piece, _ in got]
    return jnp.stack(
        [lax.select_n((place - i) % count, *pieces) for i in range(count)], axis=0
    )


def reduce_async(blocks, axis):
    got = [
        lax.ppermute(lax.dynamic_index_in_dim(blocks, target, 0, False), axis, route)
        for route, target, _ in hops(axis)
    ]
    total = lax.dynamic_index_in_dim(blocks, lax.axis_index(axis), 0, False).astype(F32)
    for piece in got:
        total = total + piece.astype(F32)
    return total


def beside(step):
    return [(i, i ^ step) for i in range(4)]


def plane_gather(block):
    if lax.axis_size("fsdp") != 4:
        return spread_async(block, "fsdp")
    half = block.shape[0] // 2
    place = lax.axis_index("fsdp")
    near = lax.ppermute(block, "fsdp", beside(1))
    side = lax.ppermute(block, "fsdp", beside(2))
    far_top = lax.ppermute(side[:half], "fsdp", beside(1))
    far_low = lax.ppermute(near[half:], "fsdp", beside(2))
    whole = jnp.zeros((4, 2, half) + block.shape[1:], block.dtype)
    parts = ((block, place), (near, place ^ 1), (side, place ^ 2))
    for piece, index in parts:
        piece = piece.reshape((1, 2, half) + block.shape[1:])
        whole = lax.dynamic_update_slice(whole, piece, (index, 0, 0, 0))
    for row, piece in enumerate((far_top, far_low)):
        whole = lax.dynamic_update_slice(whole, piece[None, None], (place ^ 3, row, 0, 0))
    return whole


def plane_reduce(make):
    def whole(target):
        return jnp.concatenate([make(target, 0), make(target, 1)], axis=0)

    if lax.axis_size("fsdp") != 4:
        sent = [(route, whole(target).astype(BF)) for route, target, _ in hops("fsdp")]
        own = whole(lax.axis_index("fsdp"))
        for route, piece in sent:
            own = own + lax.ppermute(piece, "fsdp", route).astype(F32)
        return own.astype(BF)
    place = lax.axis_index("fsdp")
    got_side = lax.ppermute(make(place ^ 3, 0).astype(BF), "fsdp", beside(1))
    got_near = lax.ppermute(make(place ^ 3, 1).astype(BF), "fsdp", beside(2))
    near_top = lax.ppermute(make(place ^ 1, 0).astype(BF), "fsdp", beside(1))
    side_low = lax.ppermute(make(place ^ 2, 1).astype(BF), "fsdp", beside(2))
    own_top = make(place, 0).astype(BF)
    own_low = make(place, 1).astype(BF)
    side_top = make(place ^ 2, 0).astype(BF)
    near_low = make(place ^ 1, 1).astype(BF)
    side_top = (side_top.astype(F32) + got_side.astype(F32)).astype(BF)
    near_low = (near_low.astype(F32) + got_near.astype(F32)).astype(BF)
    side_top = lax.ppermute(side_top, "fsdp", beside(2))
    near_low = lax.ppermute(near_low, "fsdp", beside(1))
    top = own_top.astype(F32) + near_top.astype(F32) + side_top.astype(F32)
    low = own_low.astype(F32) + near_low.astype(F32) + side_low.astype(F32)
    return jnp.concatenate([top, low], axis=0).astype(BF)


def sigmoid(values):
    return 1.0 / (1.0 + jnp.exp(-values))


def silu_grad(values, sigma):
    return sigma * (1.0 + values * (1.0 - sigma))


def rms_forward(values):
    inv_rms = lax.rsqrt(jnp.mean(values * values, axis=-1, keepdims=True) + NORM_EPS)
    return values * inv_rms, inv_rms


def rms_backward(grad_out, normed, inv_rms, gain_vec):
    grad_normed = grad_out * gain_vec[None, :]
    return inv_rms * (grad_normed - normed * jnp.mean(grad_normed * normed, axis=-1, keepdims=True))


def dot(left, right, exact=None):
    return lax.dot_general(
        left, right, (((1,), (0,)), ((), ())), precision=exact, preferred_element_type=F32
    )


def dot_nt(left, right, exact=None):
    return lax.dot_general(
        left, right, (((1,), (1,)), ((), ())), precision=exact, preferred_element_type=F32
    )


def dot_tn(left, right, exact=None):
    return lax.dot_general(
        left, right, (((0,), (0,)), ((), ())), precision=exact, preferred_element_type=F32
    )


def pad_to(array, axis, size):
    if array.shape[axis] == size:
        return array
    widths = [(0, 0)] * array.ndim
    widths[axis] = (0, size - array.shape[axis])
    return jnp.pad(array, widths)


def ceil_to(value, unit):
    return -(-value // unit) * unit


def split(values, pieces, wide=True):
    parts = []
    for _ in range(pieces):
        high = lax.reduce_precision(values, 8, 7)
        parts.append(high.astype(BF))
        values = values - high
    joined = jnp.concatenate(parts, axis=-1)
    return pad_to(joined, joined.ndim - 1, 128) if wide else joined


def fuse(values, pieces, count):
    values = values.astype(F32)
    total = values[..., :count]
    for i in range(1, pieces):
        total = total + values[..., i * count : (i + 1) * count]
    return total


class Plan:
    def __init__(self, group, rows, width, d_loc, heads, total, cc, mc):
        self.group, self.rows, self.width, self.d_loc = group, rows, width, d_loc
        self.heads, self.total, self.cc, self.mc = heads, total, cc, mc
        self.half = rows // 2
        self.chan = heads * HDIM
        self.wide = ceil_to(self.chan, 128)
        self.off = self.chan % 128
        self.conv = 2 * NSTATE + self.wide
        self.o_x = 2 * NSTATE
        self.o_v = self.o_x + self.chan
        self.o_z = ceil_to(self.o_v + HDIM, 128)
        self.o_dt = self.o_z + self.chan
        self.o_s = self.o_dt + heads
        self.n_small = KCONV + 4 + heads
        self.o_end = self.o_s + 2 * self.n_small
        self.o_q = ceil_to(self.o_end, 128)
        self.o_k = self.o_q + HDIM
        self.a_w = self.o_q + 2 * HDIM
        self.o_mo = self.a_w
        self.o_ao = self.a_w + self.chan
        self.p_w = ceil_to(self.o_ao + HDIM, 128)
        self.s_v = self.o_v - self.off
        self.s_dt = self.o_dt - self.off
        self.s_ao = self.o_ao - self.off
        self.row = self.off + heads


def lanes(count):
    return lax.broadcasted_iota(jnp.int32, (1, count), 1)


def first_rows(lengths_ref, index):
    start = jnp.zeros_like(index)
    edge = jnp.int32(0)
    for i in range(lengths_ref.shape[1] - 1):
        edge = edge + lengths_ref[0, i]
        start = jnp.where(index >= edge, edge, start)
    return start


def head_row(plan, head_ref, which):
    lane = lanes(128)
    row = jnp.zeros((1, 128), F32)
    for j in range(plan.heads):
        row = jnp.where(lane == plan.off + j, head_ref[which, j], row)
    return row


def head_wide(plan, values):
    lane = lanes(plan.wide)
    row = jnp.zeros((1, plan.wide), F32)
    for j in range(plan.heads):
        row = jnp.where(lane // HDIM == j, values[j], row)
    return row


def steps_of(plan, head_ref, slab):
    lane = lanes(128)
    live = (lane >= plan.off) & (lane < plan.row)
    shifted = jnp.where(live, slab + head_row(plan, head_ref, 0), 0.0)
    soft = jnp.maximum(shifted, 0.0) + jnp.log1p(jnp.exp(-jnp.abs(shifted)))
    dt_step = jnp.where(live, soft, 0.0)
    rate = jnp.where(live, jnp.exp(head_row(plan, head_ref, 1)), 0.0)
    return dt_step, rate, shifted, live


def small_rows(plan, w_ref, sel_ref):
    slab = w_ref[:, plan.s_dt : plan.s_dt + 128]
    turned = slab.astype(F32).T
    picked = dot_tn(slab, sel_ref[...])
    row = plan.row
    lane = lanes(plan.wide)
    taps = []
    for k in range(KCONV + 2):
        low = 2 * NSTATE + k * plan.wide
        piece = jnp.zeros((1, plan.wide), F32)
        for j in range(plan.heads):
            at = row + KCONV + 3 + j
            piece = jnp.where(lane // HDIM == j, picked[at : at + 1, low : low + plan.wide], piece)
        if k <= KCONV:
            piece = jnp.concatenate(
                [picked[row + 2 + k : row + 3 + k, : 2 * NSTATE], piece], axis=1
            )
        taps.append(piece)
    return turned[row : row + 1], turned[row + 1 : row + 2], taps


def lower_tri(group):
    return (
        lax.broadcasted_iota(jnp.int32, (group, group), 0)
        >= lax.broadcasted_iota(jnp.int32, (group, group), 1)
    ).astype(F32)


def linked_rows(plan, lengths_ref, low):
    index = lax.broadcasted_iota(jnp.int32, (plan.rows, 1), 0) + low
    start = first_rows(lengths_ref, index)
    cols = lanes(plan.group)
    return (cols <= index) & (cols >= start), index - start


def turn(values, cosine, sine):
    lane = lanes(2 * HDIM)
    moved = jnp.where(
        lane % HDIM < HDIM // 2, -pltpu.roll(values, 2 * HDIM - HDIM // 2, 1),
        pltpu.roll(values, HDIM // 2, 1),
    )
    return values * cosine + moved * sine


def split_rows(plan, values, t_id):
    low = values[: plan.half]
    high = values[plan.half :]
    return jnp.where(t_id == 0, low, high), jnp.where(t_id == 0, high, low)


def forward_kernel(
    plan, lengths_ref, head_ref, t_ref, x_ref, w_ref, sel_ref, cos_ref, sin_ref,
    keep_ref, give_ref, gain2_ref, taps_ref, norm_ref, proj_ref, pre_ref, cum_ref, ssm_ref, attn_ref, lse_ref, qk_ref,
    kq_ref, act_ref, ext_ref, dt_ref,
):
    rows, group, wide = plan.rows, plan.group, plan.wide
    gain, gain_two, taps = small_rows(plan, w_ref, sel_ref)
    gain2_ref[...] = gain_two
    for k in range(KCONV + 1):
        taps_ref[k : k + 1, :] = taps[k]
    taps_ref[KCONV + 1 : KCONV + 2, plan.o_x :] = taps[KCONV + 1]
    blocks = group // rows
    t_id = t_ref[0]
    ext_ref[0:8, :] = jnp.zeros((8, plan.conv), F32)

    lower = lower_tri(rows)

    def project(b, before):
        at = pl.ds(pl.multiple_of(b * rows, rows), rows)
        values = x_ref[at, :].astype(F32)
        normed = rms_forward(values)[0]
        norm = (normed * gain).astype(BF)
        norm_ref[at, :] = norm
        proj = dot(norm, w_ref[:, : plan.a_w])
        proj_ref[at, :] = proj
        ext_ref[pl.ds(pl.multiple_of(b * rows + 8, 8), rows), :] = (
            proj[:, : plan.conv].astype(BF).astype(F32)
        )
        rot = turn(proj[:, plan.o_q :], cos_ref[at, :], sin_ref[at, :])
        qk_ref[at, :] = rot.astype(BF)
        kq_ref[at, :] = pltpu.roll(rot, HDIM, 1).astype(BF)
        dt_step, rate, _, _ = steps_of(plan, head_ref, proj[:, plan.s_dt : plan.s_dt + 128])
        dt_ref[at, :] = dt_step
        cum = dot(lower, -dt_step * rate, EXACT) + before
        cum_ref[at, :] = cum
        return cum[rows - 1 : rows]

    lax.fori_loop(0, blocks, project, jnp.zeros((1, 128), F32))
    cum_t = cum_ref[...].T
    dt_t = dt_ref[...].T

    def convolve(b, _):
        low = pl.multiple_of(b * rows, rows)
        at = pl.ds(low, rows)
        pos = linked_rows(plan, lengths_ref, low)[1]
        ext = ext_ref[pl.ds(low, rows + 8), :]
        total = jnp.broadcast_to(taps[KCONV], (rows, plan.conv))
        for k in range(KCONV):
            step = KCONV - 1 - k
            total = total + taps[k] * (ext[8 - step : 8 - step + rows] * (pos >= step).astype(F32))
        pre_ref[at, :] = total
        act_ref[at, :] = (total * sigmoid(total)).astype(BF)
        return 0

    lax.fori_loop(0, blocks, convolve, 0)

    lane_w = lanes(wide)
    lane = lanes(128)
    in_v = (lane >= plan.off) & (lane < plan.off + HDIM)
    b_all = act_ref[:, :NSTATE]
    x_all = act_ref[:, plan.o_x : plan.o_x + wide]
    v_all = jnp.where(in_v, proj_ref[:, plan.s_v : plan.s_v + 128], 0.0).astype(BF)
    k_all = kq_ref[...]
    skip = head_wide(plan, [head_ref[2, j] for j in range(plan.heads)])
    w_m = w_ref[:, plan.o_mo : plan.o_mo + wide]
    w_o = w_ref[:, plan.s_ao : plan.s_ao + 128]

    def mix(b, _):
        low = pl.multiple_of(b * rows, rows)
        at = pl.ds(low, rows)
        linked = linked_rows(plan, lengths_ref, low)[0]
        cross = dot_nt(act_ref[at, NSTATE : 2 * NSTATE], b_all)
        cum_b = cum_ref[at, :]
        core = jnp.zeros((rows, wide), F32)
        for j in range(plan.heads):
            col = cum_b[:, plan.off + j : plan.off + j + 1]
            gaps = jnp.where(linked, col - cum_t[plan.off + j : plan.off + j + 1], -1e30)
            mixing = jnp.exp(gaps) * cross * dt_t[plan.off + j : plan.off + j + 1]
            core = jnp.where(lane_w // HDIM == j, dot(mixing.astype(BF), x_all), core)
        pre = pre_ref[at, plan.o_x : plan.o_x + wide]
        ssm = core + skip * (pre * sigmoid(pre))
        ssm_ref[at, :] = ssm
        z_gate = proj_ref[at, plan.o_z : plan.o_z + wide].astype(BF).astype(F32)
        gated = jnp.where(lane_w < plan.chan, ssm * (z_gate * sigmoid(z_gate)), 0.0)
        norm_in = (gated * taps[KCONV + 1]).astype(BF)
        square = jnp.sum(gated * gated, axis=1, keepdims=True)
        high = square.astype(BF).astype(F32)
        square = jnp.where(
            lane == 2 * t_id, high, jnp.where(lane == 2 * t_id + 1, square - high, 0.0)
        )

        query = jnp.where(lane < HDIM, qk_ref[at, :].astype(F32), 0.0).astype(BF)
        scores = jnp.where(linked, dot_nt(query, k_all) * HDIM ** (-0.5), -1e30)
        top = jnp.max(scores, axis=1, keepdims=True)
        exps = jnp.exp(scores - top)
        total = jnp.sum(exps, axis=1, keepdims=True)
        values = dot((exps / total).astype(BF), v_all).astype(BF)
        attn_ref[at, :] = values
        lse_ref[at, :] = jnp.broadcast_to(top + jnp.log(total), (rows, 128))

        out = pl.ds(pl.multiple_of(b * plan.half, plan.half), plan.half)
        width = plan.width
        for start, piece in (
            (0, dot_nt(norm_in, w_m)),
            (width, dot_nt(values, w_o)),
            (2 * width, square),
        ):
            keep, give = split_rows(plan, piece, t_id)
            keep_ref[out, start : start + piece.shape[1]] = keep.astype(BF)
            give_ref[out, start : start + piece.shape[1]] = give.astype(BF)
        return 0

    lax.fori_loop(0, blocks, mix, 0)


def backward_kernel(
    plan, lengths_ref, head_ref, t_ref, x_ref, w_ref, sel_ref, cos_ref, sin_ref,
    taps_ref, norm_ref, proj_ref, pre_ref, cum_ref, ssm_ref, attn_ref, lse_ref, qk_ref, kq_ref, got_ref,
    gain2_ref,
    keep_ref, give_ref, pack_ref,
    act_ref, ext_ref, gs_ref, ni_ref, gy_ref, ga_ref, gact_ref, gext_ref, gv_ref, gk_ref, gat_ref,
    row_ref, col_ref, dtt_ref, cumt_ref, small_ref, dt_ref,
):
    rows, group, wide, width = plan.rows, plan.group, plan.wide, plan.width
    heads, off, row = plan.heads, plan.off, plan.row
    taps = [taps_ref[k : k + 1, :] for k in range(KCONV + 1)]
    blocks = group // rows
    t_id = t_ref[0]
    lane_w = lanes(wide)
    lane = lanes(128)
    in_v = (lane >= off) & (lane < off + HDIM)
    norm_gain = taps_ref[KCONV + 1 : KCONV + 2, plan.o_x :]
    w_m = w_ref[:, plan.o_mo : plan.o_mo + wide]
    w_o = w_ref[:, plan.s_ao : plan.s_ao + 128]
    ext_ref[0:8, :] = jnp.zeros((8, plan.conv), F32)
    gext_ref[group : group + 8, :] = jnp.zeros((8, plan.conv), F32)
    skip = head_wide(plan, [head_ref[2, j] for j in range(heads)])
    scale = HDIM ** (-0.5)

    cumt_ref[...] = cum_ref[...].T

    def gate(b, sums):
        at = pl.ds(pl.multiple_of(b * rows, rows), rows)
        grad_round = got_ref[at, :width]
        factor = got_ref[at, width : width + 128].astype(F32)
        grad_rs = factor[:, 0:1] + factor[:, 2:3]
        row_scale = factor[:, 1:2] + factor[:, 3:4]
        grad_scaled = (grad_round.astype(F32) * row_scale).astype(BF)
        gs_ref[at, :] = grad_scaled
        grad_in = jnp.where(lane_w < plan.chan, dot(grad_scaled, w_m), 0.0)
        gat_ref[at, :] = jnp.where(in_v, dot(grad_round, w_o), 0.0)
        z_gate = proj_ref[at, plan.o_z : plan.o_z + wide].astype(BF).astype(F32)
        z_gate = jnp.where(lane_w < plan.chan, z_gate, 0.0)
        z_sig = sigmoid(z_gate)
        silu_z = z_gate * z_sig
        ssm = ssm_ref[at, :]
        gated = ssm * silu_z
        ni_ref[at, :] = (gated * norm_gain).astype(BF)
        grad_gated = grad_in * norm_gain - gated * (
            grad_rs * row_scale * row_scale * row_scale / plan.total
        )
        grad_y = grad_gated * silu_z
        gy_ref[at, :] = grad_y
        grad_z = grad_gated * ssm * silu_grad(z_gate, z_sig)
        ga_ref[at, plan.o_z : plan.o_z + wide] = grad_z.astype(BF)
        pre = pre_ref[at, :]
        active = pre * sigmoid(pre)
        act_ref[at, :] = active.astype(BF)
        ext_ref[pl.ds(pl.multiple_of(b * rows + 8, 8), rows), :] = (
            proj_ref[at, : plan.conv].astype(BF).astype(F32)
        )
        gact_ref[at, plan.o_x : plan.o_x + wide] = jnp.zeros((rows, wide), F32)
        gact_ref[at, :NSTATE] = jnp.zeros((rows, NSTATE), F32)
        gv_ref[at, :] = jnp.zeros((rows, 128), F32)
        gk_ref[at, :] = jnp.zeros((rows, 128), F32)
        dt_ref[at, :] = steps_of(plan, head_ref, proj_ref[at, plan.s_dt : plan.s_dt + 128])[0]
        return (
            sums[0] + jnp.sum(grad_in * gated, axis=0, keepdims=True),
            sums[1]
            + jnp.sum(grad_y * active[:, plan.o_x : plan.o_x + wide], axis=0, keepdims=True),
        )

    blank = jnp.zeros((1, wide), F32)
    g_norm_gain, skip_sum = lax.fori_loop(0, blocks, gate, (blank, blank))
    col_ref[...] = jnp.zeros((128, group), F32)
    dtt_ref[...] = dt_ref[...].T

    b_all = act_ref[:, :NSTATE]
    x_all = act_ref[:, plan.o_x : plan.o_x + wide]
    v_all = jnp.where(in_v, proj_ref[:, plan.s_v : plan.s_v + 128], 0.0).astype(BF)
    k_all = kq_ref[...]

    def mix(b, _):
        low = pl.multiple_of(b * rows, rows)
        at = pl.ds(low, rows)
        linked = linked_rows(plan, lengths_ref, low)[0]
        c_blk = act_ref[at, NSTATE : 2 * NSTATE]
        cross = dot_nt(c_blk, b_all)
        cum_b = cum_ref[at, :]
        grad_y = gy_ref[at, :]
        grad_cross = jnp.zeros((rows, group), F32)
        grad_x = jnp.zeros((group, wide), F32)
        row_slab = jnp.zeros((rows, 128), F32)
        y_round = grad_y.astype(BF)
        for j in range(heads):
            col = cum_b[:, off + j : off + j + 1]
            dt_row = dtt_ref[off + j : off + j + 1, :]
            gaps = jnp.where(linked, col - cumt_ref[off + j : off + j + 1, :], -1e30)
            decays = jnp.exp(gaps)
            weights = decays * cross
            mine = lane_w // HDIM == j
            grad_mix = dot_nt(jnp.where(mine, grad_y, 0.0).astype(BF), x_all)
            flow = grad_mix * weights
            col_ref[off + j : off + j + 1, :] += jnp.sum(flow, axis=0, keepdims=True)
            row_slab = jnp.where(
                lane == off + j, jnp.sum(flow * dt_row, axis=1, keepdims=True), row_slab
            )
            grad_cross = grad_cross + grad_mix * (decays * dt_row)
            grad_x = jnp.where(mine, dot_tn((weights * dt_row).astype(BF), y_round), grad_x)
        row_ref[at, :] = row_slab
        grad_cross = grad_cross.astype(BF)
        gact_ref[:, plan.o_x : plan.o_x + wide] += grad_x
        gact_ref[at, NSTATE : 2 * NSTATE] = dot(grad_cross, b_all)
        gact_ref[:, :NSTATE] += dot_tn(grad_cross, c_blk)

        query = jnp.where(lane < HDIM, qk_ref[at, :].astype(F32), 0.0).astype(BF)
        scores = jnp.where(linked, dot_nt(query, k_all) * scale, -1e30)
        probs = jnp.exp(scores - lse_ref[at, 0:1])
        grad_attn = gat_ref[at, :]
        delta = jnp.sum(grad_attn * attn_ref[at, :].astype(F32), axis=1, keepdims=True)
        attn_round = grad_attn.astype(BF)
        grad_prob = dot_nt(attn_round, v_all)
        grad_scores = (probs * (grad_prob - delta)).astype(BF)
        grad_q = dot(grad_scores, k_all) * scale
        gk_ref[...] += dot_tn(grad_scores, kq_ref[at, :]) * scale
        gv_ref[...] += dot_tn(probs.astype(BF), attn_round)
        gat_ref[at, :] = grad_q
        return 0

    lax.fori_loop(0, blocks, mix, 0)

    dt_ref[...] = col_ref[...].T
    lower = lower_tri(rows)

    def unwind(i, sums):
        at = pl.ds(pl.multiple_of((blocks - 1 - i) * rows, rows), rows)
        after, bias_sum, rate_sum = sums
        slab = slice(plan.s_dt, plan.s_dt + 128)
        dt_step, rate, shifted, live = steps_of(plan, head_ref, proj_ref[at, slab])
        col_slab = dt_ref[at, :]
        grad_cum = row_ref[at, :] - dt_step * col_slab
        grad_decay = dot_tn(lower, grad_cum, EXACT) + after
        grad_dt = jnp.where(live, (col_slab - rate * grad_decay) * sigmoid(shifted), 0.0)
        z_part = ga_ref[at, slab].astype(F32)
        ga_ref[at, slab] = (jnp.where(lane < off, z_part, 0.0) + grad_dt).astype(BF)
        return (
            after + jnp.sum(grad_cum, axis=0, keepdims=True),
            bias_sum + jnp.sum(grad_dt, axis=0, keepdims=True),
            rate_sum + jnp.sum(grad_decay * (-dt_step * rate), axis=0, keepdims=True),
        )

    blank = jnp.zeros((1, 128), F32)
    _, bias_sum, rate_sum = lax.fori_loop(0, blocks, unwind, (blank, blank, blank))

    def finish(b, sums):
        low = pl.multiple_of(b * rows, rows)
        at = pl.ds(low, rows)
        pre = pre_ref[at, :]
        grad_act = gact_ref[at, :]
        grad_x = grad_act[:, plan.o_x :] + skip * gy_ref[at, :]
        grad_act = jnp.concatenate([grad_act[:, : plan.o_x], grad_x], axis=1)
        grad_pre = grad_act * silu_grad(pre, sigmoid(pre))
        gext_ref[at, :] = grad_pre
        pos = linked_rows(plan, lengths_ref, low)[1]
        ext = ext_ref[pl.ds(low, rows + 8), :]
        new = []
        for k in range(KCONV):
            step = KCONV - 1 - k
            moved = ext[8 - step : 8 - step + rows] * (pos >= step).astype(F32)
            new.append(sums[k] + jnp.sum(grad_pre * moved, axis=0, keepdims=True))
        new.append(sums[KCONV] + jnp.sum(grad_pre, axis=0, keepdims=True))
        grad_q = gat_ref[at, :]
        grad_k = gk_ref[at, :]
        both = turn(jnp.where(lane < HDIM, grad_q, grad_k), cos_ref[at, :], -sin_ref[at, :])
        ga_ref[at, plan.o_q :] = both.astype(BF)
        return tuple(new)

    blank = jnp.zeros((1, plan.conv), F32)
    g_taps = lax.fori_loop(0, blocks, finish, (blank,) * (KCONV + 1))

    def close(b, total):
        low = pl.multiple_of(b * rows, rows)
        at = pl.ds(low, rows)
        ext = gext_ref[pl.ds(low, rows + 8), :]
        index = lax.broadcasted_iota(jnp.int32, (rows, 1), 0) + low
        grad_conv = jnp.zeros((rows, plan.conv), F32)
        for k in range(KCONV):
            step = KCONV - 1 - k
            later = index + step
            fits = (later - first_rows(lengths_ref, later) >= step).astype(F32)
            grad_conv = grad_conv + taps[k] * (ext[step : step + rows] * fits)
        ga_ref[at, : plan.conv] = grad_conv.astype(BF)
        v_part = jnp.where(in_v, gv_ref[at, :], 0.0)
        if plan.s_v < plan.conv:
            v_part = v_part + jnp.where(in_v, 0.0, grad_conv[:, plan.s_v : plan.s_v + 128])
        ga_ref[at, plan.s_v : plan.s_v + 128] = v_part.astype(BF)
        partial = dot_nt(ga_ref[at, :], w_ref[:, : plan.a_w])
        normed = rms_forward(x_ref[at, :].astype(F32))[0]
        keep, give = split_rows(plan, partial, t_id)
        out = pl.ds(pl.multiple_of(b * plan.half, plan.half), plan.half)
        keep_ref[out, :] = keep.astype(BF)
        give_ref[out, :] = give.astype(BF)
        return total + jnp.sum(partial * normed, axis=0, keepdims=True)

    g_gain = lax.fori_loop(0, blocks, close, jnp.zeros((1, width), F32))

    def rows_at(entries, count):
        index = lax.broadcasted_iota(jnp.int32, (128, 1), 0)
        total = jnp.zeros((128, count), F32)
        for i, value in entries:
            high = value.astype(BF).astype(F32)
            total = jnp.where(index == row + i, high, total)
            total = jnp.where(index == row + plan.n_small + i, value - high, total)
        return total

    lane_d = lanes(width) % plan.d_loc
    head_vals = jnp.zeros((1, width), F32)
    for j in range(heads):
        picks = (
            jnp.sum(jnp.where(lane == off + j, bias_sum, 0.0), axis=1, keepdims=True),
            jnp.sum(jnp.where(lane == off + j, rate_sum, 0.0), axis=1, keepdims=True),
            jnp.sum(jnp.where(lane_w // HDIM == j, skip_sum, 0.0), axis=1, keepdims=True),
        )
        for i in range(3):
            head_vals = jnp.where(lane_d == i * heads + j, picks[i], head_vals)
    direct = rows_at([(0, g_gain), (1, gain2_ref[...]), (plan.n_small - 1, head_vals)], width)
    selected = [
        rows_at([(2 + k, g_taps[k][:, : 2 * NSTATE]) for k in range(KCONV + 1)], 2 * NSTATE)
    ]
    for k in range(KCONV + 2):
        source = g_taps[k][:, plan.o_x :] if k <= KCONV else g_norm_gain
        selected.append(
            rows_at(
                [
                    (KCONV + 3 + j, jnp.where(lane_w // HDIM == j, source, 0.0))
                    for j in range(heads)
                ],
                wide,
            )
        )
    selected = jnp.concatenate(selected, axis=1).astype(BF)
    small = direct.T + dot_nt(sel_ref[...], selected)
    small_ref[...] = small
    chunk = 256

    def weigh(i, _):
        part = pl.ds(pl.multiple_of(i * chunk, chunk), chunk)
        pack_ref[part, : plan.a_w] = dot_tn(norm_ref[:, part], ga_ref[...]).astype(BF)
        slab = slice(plan.s_dt, plan.s_dt + 128)
        pack_ref[part, slab] = jnp.where(
            lane < row, pack_ref[part, slab].astype(F32), small_ref[part, :]
        ).astype(BF)
        pack_ref[part, plan.o_mo : plan.o_mo + wide] = dot_tn(
            gs_ref[:, part], ni_ref[...]
        ).astype(BF)
        slab = slice(plan.s_ao, plan.s_ao + 128)
        attn = dot_tn(got_ref[:, part], attn_ref[...])
        if plan.off:
            attn = jnp.where(in_v, attn, pack_ref[part, slab].astype(F32))
        pack_ref[part, slab] = attn.astype(BF)
        return 0

    lax.fori_loop(0, width // chunk, weigh, 0)


def call(kernel, plan, outs, scratch, scalars, arrays):
    smem = pl.BlockSpec(memory_space=pltpu.SMEM)
    vmem = pl.BlockSpec(memory_space=pltpu.VMEM)
    return pl.pallas_call(
        lambda *refs: kernel(plan, *refs),
        out_shape=[jax.ShapeDtypeStruct(shape, kind) for shape, kind in outs],
        in_specs=[smem] * len(scalars) + [vmem] * len(arrays),
        out_specs=[vmem] * len(outs),
        scratch_shapes=[pltpu.VMEM(shape, kind) for shape, kind in scratch],
        compiler_params=pltpu.CompilerParams(vmem_limit_bytes=48 << 20),
    )(*scalars, *arrays)


def per_device(
    inputs,
    seq_lengths,
    norm_gains,
    mamba_in,
    dt_proj,
    bc_proj,
    mamba_chan,
    bc_conv,
    head_params,
    query_proj,
    kv_proj,
    attn_out,
    mamba_out,
    mlp_in,
    mlp_out,
    out_grad,
):
    n_f = lax.axis_size("fsdp")
    n_c = lax.axis_size("context")
    c_id = lax.axis_index("context")
    t_id = lax.axis_index("tensor")
    shards = n_f * n_c
    rows = inputs.shape[0]
    group = rows * n_c
    half = rows // 2
    d_loc = mamba_in.shape[0]
    width = d_loc * shards
    heads_t = head_params.shape[1]
    heads = -(-heads_t // n_c)
    heads_pad = heads * n_c
    q_t = query_proj.shape[1] // HDIM
    ff = mlp_in.shape[2]
    cc = bc_conv.shape[1]
    mc = mamba_chan.shape[1]
    plan = Plan(group, rows, width, d_loc, heads, 2 * heads_t * HDIM, cc, mc)
    chan = plan.chan
    bc_w = 2 * NSTATE
    o_s, o_end, n_small, p_w = plan.o_s, plan.o_end, plan.n_small, plan.p_w

    def by_context(array, axis, count, size):
        padded = pad_to(array, axis, count * n_c * size)
        shape = padded.shape[:axis] + (n_c, count * size) + padded.shape[axis + 1 :]
        return jnp.moveaxis(padded.reshape(shape), axis, 0)

    inner_ctx = by_context(mamba_in, 2, heads, HDIM)
    query_ctx = by_context(query_proj, 1, 1, HDIM)
    dt_ctx = by_context(dt_proj, 1, heads, 1)
    chan_ctx = pad_to(jnp.swapaxes(by_context(mamba_chan, 0, heads, 1), 1, 2), 1, d_loc)
    mo_ctx = jnp.swapaxes(by_context(mamba_out, 0, heads, HDIM), 1, 2)
    ao_ctx = jnp.swapaxes(by_context(attn_out, 0, 1, HDIM), 1, 2)

    def everywhere(array):
        return jnp.broadcast_to(array[None], (n_c,) + array.shape)

    pieces = [
        (0, everywhere(bc_proj)),
        (plan.o_x, inner_ctx[:, :, 1]),
        (plan.o_v, everywhere(kv_proj[:, 1])),
        (plan.o_z, inner_ctx[:, :, 0]),
        (plan.o_dt, dt_ctx),
        (
            plan.o_s,
            everywhere(jnp.concatenate([norm_gains.T, pad_to(bc_conv.T, 0, d_loc)], axis=1)),
        ),
        (plan.o_s + KCONV + 3, chan_ctx),
        (plan.o_q, query_ctx),
        (plan.o_k, everywhere(kv_proj[:, 0])),
        (plan.o_mo, mo_ctx),
        (plan.o_ao, ao_ctx),
        (plan.p_w, None),
    ]
    columns = []
    filled = 0
    for start, piece in pieces:
        if start > filled:
            columns.append(jnp.zeros((n_c, d_loc, start - filled), BF))
        if piece is not None:
            columns.append(piece)
            filled = start + piece.shape[2]
    pack = jnp.concatenate(columns, axis=2)

    mine = lax.dynamic_slice_in_dim(inputs, t_id * half, half, 0)
    part = exchange(pack, "context").reshape(n_c * d_loc, p_w)
    got_in = spread_async(mine, "context")
    w_all = spread(part, "fsdp").reshape(width, p_w)
    rows_in = join_pair(got_in, swap_pair(got_in), t_id, 1).reshape(group, width)
    part_mi = spread_async(mlp_in.reshape(d_loc, 2 * ff), "context")
    part_mo = spread_async(mlp_out.T, "context")
    w_mi = plane_gather(part_mi.reshape(n_c * d_loc, 2 * ff)).reshape(width, 2 * ff)
    w_mo = plane_gather(part_mo.reshape(n_c * d_loc, ff)).reshape(width, ff)

    starts = jnp.cumsum(seq_lengths[0]) - seq_lengths[0]
    row_ids = jnp.arange(group, dtype=jnp.int32)
    inside = row_ids[:, None] >= starts[None, :]
    positions = row_ids - jnp.max(jnp.where(inside, starts[None, :], 0), axis=1)
    freqs = jnp.power(ROPE_BASE, -jnp.arange(HDIM // 2).astype(F32) * (2.0 / HDIM))
    angles = positions.astype(F32)[:, None] * jnp.concatenate([freqs] * 4)[None, :]
    cosine = jnp.cos(angles)
    sine = jnp.sin(angles)
    head_vec = lax.dynamic_slice_in_dim(
        pad_to(head_params, 1, heads_pad), c_id * heads, heads, 1
    )
    feature = jnp.arange(width, dtype=jnp.int32)[:, None]
    place = feature % d_loc
    shard = feature // d_loc
    lane = jnp.arange(plan.wide, dtype=jnp.int32)[None, :] % HDIM
    sel = [(place < cc) & (shard * cc + place == jnp.arange(bc_w, dtype=jnp.int32)[None, :])]
    for k in range(KCONV + 2):
        sel.append((place < mc) & (shard * mc + place == k * HDIM + lane))
    sel = jnp.concatenate(sel, axis=1).astype(BF)
    scalars = (seq_lengths, head_vec, t_id.reshape(1))
    slab_w = 2 * width + 128
    part_rows = n_c * half
    keep, give, gain_two, taps, norm, proj, pre, cum, ssm, attn, lse, qk, kq = call(
        forward_kernel,
        plan,
        [
            ((part_rows, slab_w), BF),
            ((part_rows, slab_w), BF),
            ((1, width), F32),
            ((8, plan.conv), F32),
            ((group, width), BF),
            ((group, plan.a_w), F32),
            ((group, plan.conv), F32),
            ((group, 128), F32),
            ((group, plan.wide), F32),
            ((group, 128), BF),
            ((group, 128), F32),
            ((group, 128), BF),
            ((group, 128), BF),
        ],
        [((group, plan.conv), BF), ((group + 8, plan.conv), F32), ((group, 128), F32)],
        scalars,
        (rows_in, w_all, sel, cosine, sine),
    )
    gain_mlp = gain_two[0]

    def pair_parts(values, lead):
        parts = values.reshape(lead + (2, half) + values.shape[1:])
        keep = lax.dynamic_index_in_dim(parts, t_id, len(lead), False)
        return keep, lax.dynamic_index_in_dim(parts, 1 - t_id, len(lead), False)

    def pair_sum(values, lead):
        keep, give = pair_parts(values, lead)
        return keep + swap_pair(give.astype(BF)).astype(F32)

    def pair_add(keep, give):
        return (keep.astype(F32) + swap_pair(give).astype(F32)).astype(BF)

    summed = pair_add(keep, give).reshape(n_c, half, slab_w)
    both = jnp.sum(exchange(summed, "context").astype(F32), axis=0)
    squares = jnp.sum(both[:, 2 * width : 2 * width + 4], axis=1, keepdims=True)
    scale_own = lax.rsqrt(squares / plan.total + NORM_EPS)
    mamba_own = both[:, :width]
    in_own = mine.astype(F32)
    residual = in_own + scale_own * mamba_own + both[:, width : 2 * width]

    normed_two, inv_two = rms_forward(residual)
    norm_two_own = (normed_two * gain_mlp[None, :]).astype(BF)
    norm_two = join_pair(norm_two_own, swap_pair(norm_two_own), t_id, 0).reshape(rows, width)
    stacked = jnp.concatenate([norm_two, out_grad], axis=0)
    first = dot(norm_two, w_mi)
    gate_val = first[:, :ff]
    up_val = first[:, ff:]
    grad_act = dot(out_grad, w_mo)
    gate_sig = sigmoid(gate_val)
    gate_act = gate_val * gate_sig
    mlp_act = (gate_act * up_val).astype(BF)
    grad_gate = (grad_act * up_val * silu_grad(gate_val, gate_sig)).astype(BF)
    grad_up = (grad_act * gate_act).astype(BF)
    blank = jnp.zeros((rows, ff), BF)
    mixed = jnp.concatenate(
        [
            jnp.concatenate([grad_gate, grad_up, blank], axis=1),
            jnp.concatenate([blank, blank, mlp_act], axis=1),
        ],
        axis=0,
    )
    grad_two = pair_sum(dot_nt(mixed[:rows, : 2 * ff], w_mi), ())
    top_own = lax.dynamic_slice_in_dim(out_grad, t_id * half, half, 0).astype(F32)
    g_gain_mlp = jnp.sum(grad_two * normed_two, axis=0)
    grad_res = top_own + rms_backward(grad_two, normed_two, inv_two, gain_mlp)
    grad_rs_own = jnp.sum(grad_res * mamba_own, axis=1, keepdims=True)
    factor = split(jnp.concatenate([grad_rs_own, scale_own], axis=1), 2)
    got = spread(jnp.concatenate([grad_res.astype(BF), factor], axis=1), "context")
    got = join_pair(got, swap_pair(got), t_id, 1).reshape(group, -1)
    block = n_c * d_loc

    def mlp_block(target, part):
        low = target * block + part * (block // 2)
        cols = lax.dynamic_slice_in_dim(stacked, low, block // 2, 1)
        return dot_tn(cols, mixed)

    own = plane_reduce(mlp_block)
    own = reduce_async(own.reshape(n_c, d_loc, 3 * ff), "context")
    out_mi = own[:, : 2 * ff].reshape(d_loc, 2, ff)
    out_mo = own[:, 2 * ff :].T

    keep, give, g_pack = call(
        backward_kernel,
        plan,
        [((part_rows, width), BF), ((part_rows, width), BF), ((width, p_w), BF)],
        [
            ((group, plan.conv), BF),
            ((group + 8, plan.conv), F32),
            ((group, width), BF),
            ((group, plan.wide), BF),
            ((group, plan.wide), F32),
            ((group, plan.a_w), BF),
            ((group, plan.conv), F32),
            ((group + 8, plan.conv), F32),
            ((group, 128), F32),
            ((group, 128), F32),
            ((group, 128), F32),
            ((group, 128), F32),
            ((128, group), F32),
            ((128, group), F32),
            ((128, group), F32),
            ((width, 128), F32),
            ((group, 128), F32),
        ],
        scalars,
        (
            rows_in, w_all, sel, cosine, sine, taps, norm, proj, pre, cum, ssm, attn, lse, qk, kq, got,
            g_gain_mlp[None],
        ),
    )
    mlp_act, residual, keep = lax.optimization_barrier((mlp_act, residual, keep))
    out_own = (residual + pair_sum(dot_nt(mlp_act, w_mo), ())).astype(BF)
    partial = pair_add(keep, give).reshape(n_c, half, width)
    grad_one = reduce_async(partial, "context")
    gain_mix = w_all[:, o_s].astype(F32)
    normed_own, inv_own = rms_forward(in_own)
    grad_in_own = grad_res + rms_backward(grad_one, normed_own, inv_own, gain_mix)
    output = join_pair(out_own, swap_pair(out_own), t_id, 0).reshape(rows, width)
    input_grad = join_pair(grad_in_own, swap_pair(grad_in_own), t_id, 0).reshape(rows, width)

    got = exchange(g_pack.reshape(n_f, block, p_w), "fsdp")
    got = jnp.sum(got.astype(F32), axis=0)
    g_small = fuse(got[:, o_s:o_end], 2, n_small)
    g_pack = jnp.concatenate(
        [got[:, :o_s].astype(BF), split(g_small, 2, False), got[:, o_end:].astype(BF)], axis=1
    )
    g_a = exchange(g_pack.reshape(n_c, d_loc, p_w), "context").astype(F32)

    def joined(low, size, count):
        moved = jnp.moveaxis(g_a[:, :, low : low + size], 0, 1).reshape(d_loc, n_c * size)
        return moved[:, : count]

    out_inner = jnp.stack(
        [
            joined(plan.o_z, chan, heads_t * HDIM),
            joined(plan.o_x, chan, heads_t * HDIM),
        ],
        axis=1,
    )
    out_query = joined(plan.o_q, HDIM, q_t * HDIM)
    out_dt = joined(plan.o_dt, heads, heads_t)
    out_kv = jnp.stack(
        [
            jnp.sum(g_a[:, :, plan.o_k : plan.o_k + HDIM], axis=0),
            jnp.sum(g_a[:, :, plan.o_v : plan.o_v + HDIM], axis=0),
        ],
        axis=1,
    )
    out_mout = joined(plan.o_mo, chan, heads_t * HDIM).T
    out_aout = joined(plan.o_ao, HDIM, q_t * HDIM).T
    g_small = fuse(g_a[:, :, o_s:o_end], 2, n_small)
    tail = jnp.concatenate([g_a[:, :, :bc_w], g_small[:, :, : KCONV + 3]], axis=2)
    tail = jnp.sum(tail, axis=0)
    tail = tail + swap_pair(tail)
    out_bc = tail[:, :bc_w]
    out_gains = tail[:, bc_w : bc_w + 2].T
    out_convbc = tail[:cc, bc_w + 2 :].T
    out_chan = jnp.swapaxes(g_small[:, :mc, KCONV + 3 : KCONV + 3 + heads], 1, 2)
    out_chan = out_chan.reshape(heads_pad, mc)[:heads_t]
    out_heads = g_small[:, : 3 * heads, n_small - 1].reshape(n_c, 3, heads)
    out_heads = jnp.swapaxes(out_heads, 0, 1).reshape(3, heads_pad)[:, :heads_t]

    return (
        output,
        input_grad,
        out_gains,
        out_inner,
        out_dt,
        out_bc,
        out_chan,
        out_convbc,
        out_heads,
        out_query,
        out_kv,
        out_aout,
        out_mout,
        out_mi,
        out_mo,
    )


def solution(mesh):
    both = ("fsdp", "context")
    rows = P(both, None)

    return jax.shard_map(
        per_device,
        mesh=mesh,
        in_specs=(
            rows,
            P("fsdp", None),
            P(None, both),
            P(both, None, "tensor"),
            P(both, "tensor"),
            rows,
            P("tensor", both),
            P(None, both),
            P(None, "tensor"),
            P(both, "tensor"),
            P(both, None, "tensor"),
            P("tensor", both),
            P("tensor", both),
            P(both, None, "tensor"),
            P("tensor", both),
            rows,
        ),
        out_specs=(
            rows,
            rows,
            P(None, both),
            P(both, None, "tensor"),
            P(both, "tensor"),
            rows,
            P("tensor", both),
            P(None, both),
            P(None, "tensor"),
            P(both, "tensor"),
            P(both, None, "tensor"),
            P("tensor", both),
            P("tensor", both),
            P(both, None, "tensor"),
            P("tensor", both),
        ),
        check_vma=False,
    )
```

profile of v0, /device:TPU:0, one launch (start us, length us, event | category | flops | bytes accessed | tf_op | source)
XLA Modules:
  0.0 338.1 jit_solution(3512435737973288365)
XLA Ops:
  1.7 5.1 %collective-permute-start.2 = (bf16[64,1024]{1,0:T(8,128)(2,1)S(1)}, bf16[64,1024]{1,0:T(8,128)(2,1)S(1)}, u32[]{:S(2)}, u32[]{:S(2)}) collective-permute-start(bf16[64,1024]{1,0:T(8,128)(2,1)S(1)} %get-tuple-element.163), channel_id=1, source_target_pairs={{0,6},{2,0},{4,2},{6,4},{1,7},{3,1},{5,3},{7,5},{8,14},{10,8},{12,... | collective-permute-start | bytes 393224 | tf_op jit(solution)/shard_map/ppermute | solution.py:47
  21.6 3.5 %all-to-all-start = ((bf16[4,64,1152]{2,1,0:T(8,128)(2,1)}), bf16[4,64,1152]{2,1,0:T(8,128)(2,1)S(1)}, u32[]{:S(2)}, u32[]{:S(2)}) async-start(bf16[4,64,1152]{2,1,0:T(8,128)(2,1)} %concatenate.48), calls=%async_computation | async-start | bytes 1179648 | tf_op jit(solution)/shard_map/all_to_all | solution.py:30
  28.6 11.2 %all-to-all-done = bf16[4,64,1152]{2,1,0:T(8,128)(2,1)S(1)} async-done(((bf16[4,64,1152]{2,1,0:T(8,128)(2,1)}), bf16[4,64,1152]{2,1,0:T(8,128)(2,1)S(1)}, u32[]{:S(2)}, u32[]{:S(2)}) %all-to-all-start) | async-done | bytes 589856 | tf_op jit(solution)/shard_map/all_to_all | solution.py:30
  41.4 4.6 %all-to-all-start.1 = ((bf16[4,256,1152]{2,1,0:T(8,128)(2,1)}), bf16[4,256,1152]{2,1,0:T(8,128)(2,1)}, u32[]{:S(2)}, u32[]{:S(2)}) async-start(bf16[4,256,1152]{2,1,0:T(8,128)(2,1)} %broadcast_in_dim.101), calls=%async_computation.1 | async-start | bytes 4718592 | tf_op jit(solution)/shard_map/all_to_all | solution.py:30
  48.0 3.7 %collective-permute-start.8 = (bf16[64,2048]{1,0:T(8,128)(2,1)}, bf16[64,2048]{1,0:T(8,128)(2,1)}, u32[]{:S(2)}, u32[]{:S(2)}) collective-permute-start(bf16[64,2048]{1,0:T(8,128)(2,1)} %bitcast.109), channel_id=1, source_target_pairs={{0,6},{2,0},{4,2},{6,4},{1,7},{3,1},{5,3},{7,5},{8,14},{10,8},{12,... | collective-permute-start | bytes 786440 | tf_op jit(solution)/shard_map/ppermute | solution.py:47
  61.8 12.5 %all-to-all-done.1 = bf16[4,256,1152]{2,1,0:T(8,128)(2,1)} async-done(((bf16[4,256,1152]{2,1,0:T(8,128)(2,1)}), bf16[4,256,1152]{2,1,0:T(8,128)(2,1)}, u32[]{:S(2)}, u32[]{:S(2)}) %all-to-all-start.1) | async-done | bytes 2359328 | tf_op jit(solution)/shard_map/all_to_all | solution.py:30
  74.2 14.4 %shard_map.271 = (bf16[256,2176]{1,0:T(8,128)(2,1)}, bf16[256,2176]{1,0:T(8,128)(2,1)}, f32[1,1024]{1,0:T(1,128)S(1)}, f32[8,512]{1,0:T(8,128)S(1)}, bf16[512,10...) custom-call(s32[1,2]{1,0:T(1,128)S(1)} %copy-done.14, ...), custom_call_target="tpu_custom_call" | custom-call | tf_op jit(solution)/shard_map/pallas_call | solution.py:684
  108.1 4.3 %all-to-all-start.2 = ((bf16[4,64,2176]{2,1,0:T(8,128)(2,1)}), bf16[4,64,2176]{2,1,0:T(8,128)(2,1)}, u32[]{:S(2)}, u32[]{:S(2)}) async-start(bf16[4,64,2176]{2,1,0:T(8,128)(2,1)} %bitcast.210), calls=%async_computation.2 | async-start | bytes 2228224 | tf_op jit(solution)/shard_map/all_to_all | solution.py:30
  116.1 16.8 %collective-permute-done.18 = bf16[128,1024]{1,0:T(8,128)(2,1)} collective-permute-done((bf16[128,1024]{1,0:T(8,128)(2,1)}, bf16[128,1024]{1,0:T(8,128)(2,1)}, u32[]{:S(2)}, u32[]{:S(2)}) %collective-permute-start.18) | collective-permute-done | bytes 262176 | tf_op jit(solution)/shard_map/ppermute | solution.py:83
  145.2 3.9 %collective-permute-done.11 = bf16[128,2048]{1,0:T(8,128)(2,1)S(1)} collective-permute-done((bf16[128,2048]{1,0:T(8,128)(2,1)S(1)}, bf16[128,2048]{1,0:T(8,128)(2,1)S(1)}, u32[]{:S(2)}, u32[]{:S(2)}) %collective-permute-start.11) | collective-permute-done | bytes 524320 | tf_op jit(solution)/shard_map/ppermute | solution.py:83
  159.1 4.0 %fusion.96 = f32[2,64,1024]{2,1,0:T(8,128)S(1)} fusion(bf16[2,64,2048]{2,1,0:T(8,128)(2,1)S(1)} %bitcast.216, bf16[1024,2048,1]{1,0,2:T(8,128)(2,1)} %bitcast.53), kind=kOutput, calls=%fused_computation.239 | convolution fusion | flops 536870912 | bytes 5242880 | tf_op jit(solution)/shard_map/dot_general | solution.py:148
  174.1 4.4 %all-to-all-start.3 = ((bf16[4,64,1152]{2,1,0:T(8,128)(2,1)}), bf16[4,64,1152]{2,1,0:T(8,128)(2,1)}, u32[]{:S(2)}, u32[]{:S(2)}) async-start(bf16[4,64,1152]{2,1,0:T(8,128)(2,1)} %broadcast_in_dim.110), calls=%async_computation.3 | async-start | bytes 1179648 | tf_op jit(solution)/shard_map/all_to_all | solution.py:30
  178.6 8.6 %collective-permute-done.31 = bf16[128,3072]{1,0:T(8,128)(2,1)} collective-permute-done((bf16[128,3072]{1,0:T(8,128)(2,1)}, bf16[128,3072]{1,0:T(8,128)(2,1)}, u32[]{:S(2)}, u32[]{:S(2)}) %collective-permute-start.31) | collective-permute-done | bytes 786464 | tf_op jit(solution)/shard_map/ppermute | solution.py:106
  200.6 3.5 %collective-permute-done.30 = bf16[128,3072]{1,0:T(8,128)(2,1)} collective-permute-done((bf16[128,3072]{1,0:T(8,128)(2,1)}, bf16[128,3072]{1,0:T(8,128)(2,1)}, u32[]{:S(2)}, u32[]{:S(2)}) %collective-permute-start.30) | collective-permute-done | bytes 786464 | tf_op jit(solution)/shard_map/ppermute | solution.py:108
  204.1 6.7 %collective-permute-done.32 = bf16[128,3072]{1,0:T(8,128)(2,1)} collective-permute-done((bf16[128,3072]{1,0:T(8,128)(2,1)}, bf16[128,3072]{1,0:T(8,128)(2,1)}, u32[]{:S(2)}, u32[]{:S(2)}) %collective-permute-start.32) | collective-permute-done | bytes 786464 | tf_op jit(solution)/shard_map/ppermute | solution.py:116
  212.8 12.3 %collective-permute-done.35 = bf16[128,3072]{1,0:T(8,128)(2,1)} collective-permute-done((bf16[128,3072]{1,0:T(8,128)(2,1)}, bf16[128,3072]{1,0:T(8,128)(2,1)}, u32[]{:S(2)}, u32[]{:S(2)}) %collective-permute-start.35) | collective-permute-done | bytes 786464 | tf_op jit(solution)/shard_map/ppermute | solution.py:109
  231.0 22.6 %shard_map.272 = (bf16[256,1024]{1,0:T(8,128)(2,1)S(1)}, bf16[256,1024]{1,0:T(8,128)(2,1)S(1)}, bf16[1024,1152]{1,0:T(8,128)(2,1)}) custom-call(s32[1,2]{1,0:T(1,128)S(1)} %copy-done.14, f32[3,3]{1,0:T(4,128)S(1)} %constant_dynamic-slice_fusion.refs_1_, s32[1]{0:T(128)} %bitcast.refs_2_, bf16[512,1024]{1,0:T(8,128)(2,1)S(1)} %bitcast.199, ...), custom_call_target="tpu_custom_call" | custom-call | tf_op jit(solution)/shard_map/pallas_call | solution.py:684
  255.2 3.8 %all-to-all-start.4 = ((bf16[4,256,1152]{2,1,0:T(8,128)(2,1)}), bf16[4,256,1152]{2,1,0:T(8,128)(2,1)S(1)}, u32[]{:S(2)}, u32[]{:S(2)}) async-start(bf16[4,256,1152]{2,1,0:T(8,128)(2,1)} %bitcast.214), calls=%async_computation.4 | async-start | bytes 4718592 | tf_op jit(solution)/shard_map/all_to_all | solution.py:30
  263.6 3.5 %collective-permute-start.38 = (bf16[64,3072]{1,0:T(8,128)(2,1)}, bf16[64,3072]{1,0:T(8,128)(2,1)}, u32[]{:S(2)}, u32[]{:S(2)}) collective-permute-start(bf16[64,3072]{1,0:T(8,128)(2,1)} %get-tuple-element.169), channel_id=1, source_target_pairs={{0,6},{2,0},{4,2},{6,4},{1,7},{3,1},{5,3},{7,5},{8,14},{10,8},{12,... | collective-permute-start | bytes 1179656 | tf_op jit(solution)/shard_map/ppermute | solution.py:63
  267.6 3.8 %collective-permute-start.27 = (bf16[64,1024]{1,0:T(8,128)(2,1)S(1)}, bf16[64,1024]{1,0:T(8,128)(2,1)S(1)}, u32[]{:S(2)}, u32[]{:S(2)}) collective-permute-start(bf16[64,1024]{1,0:T(8,128)(2,1)S(1)} %get-tuple-element.192), channel_id=1, source_target_pairs={{0,6},{2,0},{4,2},{6,4},{1,7},{3,1},{5,3},{7,5},{8,14},{10,8},{12,... | collective-permute-start | bytes 393224 | tf_op jit(solution)/shard_map/ppermute | solution.py:63
  272.2 16.4 %collective-permute-done.25 = bf16[64,1024]{1,0:T(8,128)(2,1)S(1)} collective-permute-done((bf16[64,1024]{1,0:T(8,128)(2,1)S(1)}, bf16[64,1024]{1,0:T(8,128)(2,1)S(1)}, u32[]{:S(2)}, u32[]{:S(2)}) %collective-permute-start.25) | collective-permute-done | bytes 131104 | tf_op jit(solution)/shard_map/ppermute | solution.py:63
  291.1 13.5 %collective-permute-done.26 = bf16[64,1024]{1,0:T(8,128)(2,1)S(1)} collective-permute-done((bf16[64,1024]{1,0:T(8,128)(2,1)S(1)}, bf16[64,1024]{1,0:T(8,128)(2,1)S(1)}, u32[]{:S(2)}, u32[]{:S(2)}) %collective-permute-start.26) | collective-permute-done | bytes 131104 | tf_op jit(solution)/shard_map/ppermute | solution.py:63
  307.4 3.7 %all-to-all-start.5 = ((bf16[4,64,1152]{2,1,0:T(8,128)(2,1)}), bf16[4,64,1152]{2,1,0:T(8,128)(2,1)S(1)}, u32[]{:S(2)}, u32[]{:S(2)}) async-start(bf16[4,64,1152]{2,1,0:T(8,128)(2,1)} %bitcast.79), calls=%async_computation.5 | async-start | bytes 1179648 | tf_op jit(solution)/shard_map/all_to_all | solution.py:30
  318.1 9.6 %all-to-all-done.5 = bf16[4,64,1152]{2,1,0:T(8,128)(2,1)S(1)} async-done(((bf16[4,64,1152]{2,1,0:T(8,128)(2,1)}), bf16[4,64,1152]{2,1,0:T(8,128)(2,1)S(1)}, u32[]{:S(2)}, u32[]{:S(2)}) %all-to-all-start.5) | async-done | bytes 589856 | tf_op jit(solution)/shard_map/all_to_all | solution.py:30
  (345 shorter events, 139.6 us)
Async XLA Ops:
  1.7 46.0 %collective-permute-start.2 = (bf16[64,1024]{1,0:T(8,128)(2,1)S(1)}, bf16[64,1024]{1,0:T(8,128)(2,1)S(1)}, u32[]{:S(2)}, u32[]{:S(2)}) collective-permute-start(bf16[64,1024]{1,0:T(8,128)(2,1)S(1)} %get-tuple-element.163), channel_id=1, source_target_pairs={{0,6},{2,0},{4,2},{6,4},{1,7},{3,1},{5,3},{7,5},{8,14},{10,8},{12,... | collective-permute-start | bytes 393224 | tf_op jit(solution)/shard_map/ppermute | solution.py:47
  6.9 41.1 %collective-permute-start.1 = (bf16[64,1024]{1,0:T(8,128)(2,1)S(1)}, bf16[64,1024]{1,0:T(8,128)(2,1)S(1)}, u32[]{:S(2)}, u32[]{:S(2)}) collective-permute-start(bf16[64,1024]{1,0:T(8,128)(2,1)S(1)} %get-tuple-element.163), channel_id=1, source_target_pairs={{0,4},{2,6},{4,0},{6,2},{1,5},{3,7},{5,1},{7,3},{8,12},{10,14},{12... | collective-permute-start | bytes 393224 | tf_op jit(solution)/shard_map/ppermute | solution.py:47
  6.9 44.8 %collective-permute-start = (bf16[64,1024]{1,0:T(8,128)(2,1)S(1)}, bf16[64,1024]{1,0:T(8,128)(2,1)S(1)}, u32[]{:S(2)}, u32[]{:S(2)}) collective-permute-start(bf16[64,1024]{1,0:T(8,128)(2,1)S(1)} %get-tuple-element.163), channel_id=1, source_target_pairs={{0,2},{2,4},{4,6},{6,0},{1,3},{3,5},{5,7},{7,1},{8,10},{10,12},{12... | collective-permute-start | bytes 393224 | tf_op jit(solution)/shard_map/ppermute | solution.py:47
  7.9 48.0 %collective-permute-start.14 = (bf16[64,1024]{1,0:T(8,128)(2,1)}, bf16[64,1024]{1,0:T(8,128)(2,1)}, u32[]{:S(2)}, u32[]{:S(2)}) collective-permute-start(bf16[64,1024]{1,0:T(8,128)(2,1)} %bitcast.39), channel_id=1, source_target_pairs={{0,4},{2,6},{4,0},{6,2},{1,5},{3,7},{5,1},{7,3},{8,12},{10,14},{12... | collective-permute-start | bytes 393224 | tf_op jit(solution)/shard_map/ppermute | solution.py:47
  9.8 46.1 %collective-permute-start.15 = (bf16[64,1024]{1,0:T(8,128)(2,1)}, bf16[64,1024]{1,0:T(8,128)(2,1)}, u32[]{:S(2)}, u32[]{:S(2)}) collective-permute-start(bf16[64,1024]{1,0:T(8,128)(2,1)} %bitcast.39), channel_id=1, source_target_pairs={{0,6},{2,0},{4,2},{6,4},{1,7},{3,1},{5,3},{7,5},{8,14},{10,8},{12,... | collective-permute-start | bytes 393224 | tf_op jit(solution)/shard_map/ppermute | solution.py:47
  41.4 32.9 %all-to-all-start.1 = ((bf16[4,256,1152]{2,1,0:T(8,128)(2,1)}), bf16[4,256,1152]{2,1,0:T(8,128)(2,1)}, u32[]{:S(2)}, u32[]{:S(2)}) async-start(bf16[4,256,1152]{2,1,0:T(8,128)(2,1)} %broadcast_in_dim.101), calls=%async_computation.1 | async-start | bytes 4718592 | tf_op jit(solution)/shard_map/all_to_all | solution.py:30
  48.0 42.4 %collective-permute-start.8 = (bf16[64,2048]{1,0:T(8,128)(2,1)}, bf16[64,2048]{1,0:T(8,128)(2,1)}, u32[]{:S(2)}, u32[]{:S(2)}) collective-permute-start(bf16[64,2048]{1,0:T(8,128)(2,1)} %bitcast.109), channel_id=1, source_target_pairs={{0,6},{2,0},{4,2},{6,4},{1,7},{3,1},{5,3},{7,5},{8,14},{10,8},{12,... | collective-permute-start | bytes 786440 | tf_op jit(solution)/shard_map/ppermute | solution.py:47
  55.8 35.2 %collective-permute-start.7 = (bf16[64,2048]{1,0:T(8,128)(2,1)}, bf16[64,2048]{1,0:T(8,128)(2,1)}, u32[]{:S(2)}, u32[]{:S(2)}) collective-permute-start(bf16[64,2048]{1,0:T(8,128)(2,1)} %bitcast.109), channel_id=1, source_target_pairs={{0,4},{2,6},{4,0},{6,2},{1,5},{3,7},{5,1},{7,3},{8,12},{10,14},{12... | collective-permute-start | bytes 786440 | tf_op jit(solution)/shard_map/ppermute | solution.py:47
  55.9 35.1 %collective-permute-start.6 = (bf16[64,2048]{1,0:T(8,128)(2,1)}, bf16[64,2048]{1,0:T(8,128)(2,1)}, u32[]{:S(2)}, u32[]{:S(2)}) collective-permute-start(bf16[64,2048]{1,0:T(8,128)(2,1)} %bitcast.109), channel_id=1, source_target_pairs={{0,2},{2,4},{4,6},{6,0},{1,3},{3,5},{5,7},{7,1},{8,10},{10,12},{12... | collective-permute-start | bytes 786440 | tf_op jit(solution)/shard_map/ppermute | solution.py:47
  59.5 40.9 %collective-permute-start.17 = (bf16[256,1024]{1,0:T(8,128)(2,1)}, bf16[256,1024]{1,0:T(8,128)(2,1)}, u32[]{:S(2)}, u32[]{:S(2)}) collective-permute-start(bf16[256,1024]{1,0:T(8,128)(2,1)} %bitcast.45), channel_id=1, source_target_pairs={{0,16},{8,24},{16,0},{24,8},{1,17},{9,25},{17,1},{25,9},{2,18},{10... | collective-permute-start | bytes 1572872 | tf_op jit(solution)/shard_map/ppermute | solution.py:82
  93.5 41.1 %collective-permute-start.10 = (bf16[256,2048]{1,0:T(8,128)(2,1)}, bf16[256,2048]{1,0:T(8,128)(2,1)}, u32[]{:S(2)}, u32[]{:S(2)}) collective-permute-start(bf16[256,2048]{1,0:T(8,128)(2,1)} %bitcast.33), channel_id=1, source_target_pairs={{0,16},{8,24},{16,0},{24,8},{1,17},{9,25},{17,1},{25,9},{2,18},{10... | collective-permute-start | bytes 3145736 | tf_op jit(solution)/shard_map/ppermute | solution.py:82
  94.1 44.0 %collective-permute-start.9 = (bf16[256,2048]{1,0:T(8,128)(2,1)}, bf16[256,2048]{1,0:T(8,128)(2,1)}, u32[]{:S(2)}, u32[]{:S(2)}) collective-permute-start(bf16[256,2048]{1,0:T(8,128)(2,1)} %bitcast.33), channel_id=1, source_target_pairs={{0,8},{8,0},{16,24},{24,16},{1,9},{9,1},{17,25},{25,17},{2,10},{10... | collective-permute-start | bytes 3145736 | tf_op jit(solution)/shard_map/ppermute | solution.py:81
  102.1 30.9 %collective-permute-start.18 = (bf16[128,1024]{1,0:T(8,128)(2,1)}, bf16[128,1024]{1,0:T(8,128)(2,1)}, u32[]{:S(2)}, u32[]{:S(2)}) collective-permute-start(bf16[128,1024]{1,0:T(8,128)(2,1)} %slice.167), channel_id=1, source_target_pairs={{0,8},{8,0},{16,24},{24,16},{1,9},{9,1},{17,25},{25,17},{2,10},{10... | collective-permute-start | bytes 786440 | tf_op jit(solution)/shard_map/ppermute | solution.py:83
  106.2 30.2 %collective-permute-start.19 = (bf16[128,1024]{1,0:T(8,128)(2,1)}, bf16[128,1024]{1,0:T(8,128)(2,1)}, u32[]{:S(2)}, u32[]{:S(2)}) collective-permute-start(bf16[128,1024]{1,0:T(8,128)(2,1)} %slice.168), channel_id=1, source_target_pairs={{0,16},{8,24},{16,0},{24,8},{1,17},{9,25},{17,1},{25,9},{2,18},{10... | collective-permute-start | bytes 786440 | tf_op jit(solution)/shard_map/ppermute | solution.py:84
  108.1 41.9 %all-to-all-start.2 = ((bf16[4,64,2176]{2,1,0:T(8,128)(2,1)}), bf16[4,64,2176]{2,1,0:T(8,128)(2,1)}, u32[]{:S(2)}, u32[]{:S(2)}) async-start(bf16[4,64,2176]{2,1,0:T(8,128)(2,1)} %bitcast.210), calls=%async_computation.2 | async-start | bytes 2228224 | tf_op jit(solution)/shard_map/all_to_all | solution.py:30
  165.9 29.2 %collective-permute-start.33 = (bf16[128,3072]{1,0:T(8,128)(2,1)}, bf16[128,3072]{1,0:T(8,128)(2,1)}, u32[]{:S(2)}, u32[]{:S(2)}) collective-permute-start(bf16[128,3072]{1,0:T(8,128)(2,1)} %convolution_convert_fusion.1), channel_id=1, source_target_pairs={{0,16},{8,24},{16,0},{24,8},{1,17},{9,25},{17,1},{25,9},{2,18},{10... | collective-permute-start | bytes 2359304 | tf_op jit(solution)/shard_map/ppermute | solution.py:107
  169.2 34.9 %collective-permute-start.30 = (bf16[128,3072]{1,0:T(8,128)(2,1)}, bf16[128,3072]{1,0:T(8,128)(2,1)}, u32[]{:S(2)}, u32[]{:S(2)}) collective-permute-start(bf16[128,3072]{1,0:T(8,128)(2,1)} %convolution_convert_fusion.6), channel_id=1, source_target_pairs={{0,8},{8,0},{16,24},{24,16},{1,9},{9,1},{17,25},{25,17},{2,10},{10... | collective-permute-start | bytes 2359304 | tf_op jit(solution)/shard_map/ppermute | solution.py:108
  194.6 30.6 %collective-permute-start.35 = (bf16[128,3072]{1,0:T(8,128)(2,1)}, bf16[128,3072]{1,0:T(8,128)(2,1)}, u32[]{:S(2)}, u32[]{:S(2)}) collective-permute-start(bf16[128,3072]{1,0:T(8,128)(2,1)} %convolution_convert_fusion), channel_id=1, source_target_pairs={{0,16},{8,24},{16,0},{24,8},{1,17},{9,25},{17,1},{25,9},{2,18},{10... | collective-permute-start | bytes 2359304 | tf_op jit(solution)/shard_map/ppermute | solution.py:109
  197.6 27.6 %collective-permute-start.34 = (bf16[128,3072]{1,0:T(8,128)(2,1)}, bf16[128,3072]{1,0:T(8,128)(2,1)}, u32[]{:S(2)}, u32[]{:S(2)}) collective-permute-start(bf16[128,3072]{1,0:T(8,128)(2,1)} %add_convert_fusion.2), channel_id=1, source_target_pairs={{0,8},{8,0},{16,24},{24,16},{1,9},{9,1},{17,25},{25,17},{2,10},{10... | collective-permute-start | bytes 2359304 | tf_op jit(solution)/shard_map/ppermute | solution.py:117
  200.5 28.0 %collective-permute-start.21 = (bf16[4,64,1152]{2,1,0:T(8,128)(2,1)}, bf16[4,64,1152]{2,1,0:T(8,128)(2,1)S(1)}, u32[]{:S(2)}, u32[]{:S(2)}) collective-permute-start(bf16[4,64,1152]{2,1,0:T(8,128)(2,1)} %all-to-all-done.3), channel_id=1, source_target_pairs={{0,1},{1,0},{2,3},{3,2},{4,5},{5,4},{6,7},{7,6},{8,9},{9,8},{10,11... | collective-permute-start | bytes 1769480 | tf_op jit(solution)/shard_map/ppermute | solution.py:20
  255.2 49.9 %all-to-all-start.4 = ((bf16[4,256,1152]{2,1,0:T(8,128)(2,1)}), bf16[4,256,1152]{2,1,0:T(8,128)(2,1)S(1)}, u32[]{:S(2)}, u32[]{:S(2)}) async-start(bf16[4,256,1152]{2,1,0:T(8,128)(2,1)} %bitcast.214), calls=%async_computation.4 | async-start | bytes 4718592 | tf_op jit(solution)/shard_map/all_to_all | solution.py:30
  263.3 47.9 %collective-permute-start.36 = (bf16[64,3072]{1,0:T(8,128)(2,1)}, bf16[64,3072]{1,0:T(8,128)(2,1)S(1)}, u32[]{:S(2)}, u32[]{:S(2)}) collective-permute-start(bf16[64,3072]{1,0:T(8,128)(2,1)} %get-tuple-element.168), channel_id=1, source_target_pairs={{0,2},{2,4},{4,6},{6,0},{1,3},{3,5},{5,7},{7,1},{8,10},{10,12},{12... | collective-permute-start | bytes 1179656 | tf_op jit(solution)/shard_map/ppermute | solution.py:63
  263.6 47.6 %collective-permute-start.38 = (bf16[64,3072]{1,0:T(8,128)(2,1)}, bf16[64,3072]{1,0:T(8,128)(2,1)}, u32[]{:S(2)}, u32[]{:S(2)}) collective-permute-start(bf16[64,3072]{1,0:T(8,128)(2,1)} %get-tuple-element.169), channel_id=1, source_target_pairs={{0,6},{2,0},{4,2},{6,4},{1,7},{3,1},{5,3},{7,5},{8,14},{10,8},{12,... | collective-permute-start | bytes 1179656 | tf_op jit(solution)/shard_map/ppermute | solution.py:63
  271.4 33.1 %collective-permute-start.26 = (bf16[64,1024]{1,0:T(8,128)(2,1)S(1)}, bf16[64,1024]{1,0:T(8,128)(2,1)S(1)}, u32[]{:S(2)}, u32[]{:S(2)}) collective-permute-start(bf16[64,1024]{1,0:T(8,128)(2,1)S(1)} %get-tuple-element.193), channel_id=1, source_target_pairs={{0,4},{2,6},{4,0},{6,2},{1,5},{3,7},{5,1},{7,3},{8,12},{10,14},{12... | collective-permute-start | bytes 393224 | tf_op jit(solution)/shard_map/ppermute | solution.py:63
  (72 other events, 956.9 us)
where the time goes:
time: 340 us; the launch traced here: 338 us
  waiting for transfers between devices  120 us (35%)
  starting transfers between devices  65.1 us (19%)
  local copies, waits for them, and re-layouts  54.9 us (16%)
  Pallas kernels  37.1 us (11%)
  other arithmetic  35.2 us (10%)
  matrix products  24.1 us (7%)
    pallas_call x2, Pallas kernels, call(): pl.pallas_call(lambda *refs: kernel(plan, *refs), out_shape=[jax.ShapeDty...  37.1 us
    all_to_all x6, waiting for transfers between devices, exchange(): return lax.all_to_all(blocks, axis, 0, 0, tiled=True)  33.3 us
    ppermute x6, waiting for transfers between devices, reduce_async(): lax.ppermute(lax.dynamic_index_in_dim(blocks, target, 0, False), axis, ro...  31.5 us
    all_to_all x6, starting transfers between devices, exchange(): return lax.all_to_all(blocks, axis, 0, 0, tiled=True)  24.3 us
    ppermute x2, waiting for transfers between devices, plane_gather(): far_top = lax.ppermute(side[:half], 'fsdp', beside(1))  20.7 us
    ppermute x9, starting transfers between devices, spread_async(): lax.ppermute(block, axis, route)  16.5 us
    dot_general x8, matrix products, dot_tn(): lax.dot_general(left, right, (((0,), (0,)), ((), ())), precision=exact, p...  13.9 us
    ppermute x1, waiting for transfers between devices, plane_reduce(): side_low = lax.ppermute(make(place ^ 2, 1).astype(BF), 'fsdp', beside(2))  12.3 us
  transfers between devices with their start and end apart: 45, of which 14 were waited for; matrix products, arithmetic and copies ran while one was open for 28% of the time, Pallas kernels for 4%

commit v1 on v0

--- a/solution.py
+++ b/solution.py
@@ -176,14 +176,6 @@
         values = values - high
     joined = jnp.concatenate(parts, axis=-1)
     return pad_to(joined, joined.ndim - 1, 128) if wide else joined
-
-
-def fuse(values, pieces, count):
-    values = values.astype(F32)
-    total = values[..., :count]
-    for i in range(1, pieces):
-        total = total + values[..., i * count : (i + 1) * count]
-    return total
 
 
 class Plan:
@@ -303,13 +295,34 @@
     return jnp.where(t_id == 0, low, high), jnp.where(t_id == 0, high, low)
 
 
+def views(plan, trig_ref, wide_ref, thin_ref):
+    def part(ref, low, size):
+        return ref.at[:, low : low + size]
+
+    wide = plan.wide
+    return (
+        part(trig_ref, 0, 128),
+        part(trig_ref, 128, 128),
+        part(wide_ref, 0, wide),
+        part(wide_ref, wide, 128),
+        part(wide_ref, wide + 128, 128),
+        part(thin_ref, 0, 128),
+        part(thin_ref, 128, 128),
+        part(thin_ref, 256, 128),
+    )
+
+
 def forward_kernel(
-    plan, lengths_ref, head_ref, t_ref, x_ref, w_ref, sel_ref, cos_ref, sin_ref,
-    keep_ref, give_ref, gain2_ref, taps_ref, norm_ref, proj_ref, pre_ref, cum_ref, ssm_ref, attn_ref, lse_ref, qk_ref,
-    kq_ref, act_ref, ext_ref, dt_ref,
+    plan, lengths_ref, head_ref, t_ref, x_ref, w_ref, sel_ref, trig_ref,
+    keep_ref, give_ref, gain1_ref, gain2_ref, taps_ref, norm_ref, proj_ref, pre_ref, wide_ref, thin_ref,
+    act_ref, ext_ref, dt_ref,
 ):
+    cos_ref, sin_ref, ssm_ref, cum_ref, lse_ref, attn_ref, qk_ref, kq_ref = views(
+        plan, trig_ref, wide_ref, thin_ref
+    )
     rows, group, wide = plan.rows, plan.group, plan.wide
     gain, gain_two, taps = small_rows(plan, w_ref, sel_ref)
+    gain1_ref[...] = gain
     gain2_ref[...] = gain_two
     for k in range(KCONV + 1):
         taps_ref[k : k + 1, :] = taps[k]
@@ -419,13 +432,16 @@
 
 
 def backward_kernel(
-    plan, lengths_ref, head_ref, t_ref, x_ref, w_ref, sel_ref, cos_ref, sin_ref,
-    taps_ref, norm_ref, proj_ref, pre_ref, cum_ref, ssm_ref, attn_ref, lse_ref, qk_ref, kq_ref, got_ref,
-    gain2_ref,
+    plan, lengths_ref, head_ref, t_ref, x_ref, w_ref, sel_ref, trig_ref,
+    taps_ref, norm_ref, proj_ref, pre_ref, wide_ref, thin_ref, mine_ref,
+    other_ref, gain2_ref,
     keep_ref, give_ref, pack_ref,
     act_ref, ext_ref, gs_ref, ni_ref, gy_ref, ga_ref, gact_ref, gext_ref, gv_ref, gk_ref, gat_ref,
-    row_ref, col_ref, dtt_ref, cumt_ref, small_ref, dt_ref,
+    row_ref, col_ref, dtt_ref, cumt_ref, small_ref, dt_ref, got_ref,
 ):
+    cos_ref, sin_ref, ssm_ref, cum_ref, lse_ref, attn_ref, qk_ref, kq_ref = views(
+        plan, trig_ref, wide_ref, thin_ref
+    )
     rows, group, wide, width = plan.rows, plan.group, plan.wide, plan.width
     heads, off, row = plan.heads, plan.off, plan.row
     taps = [taps_ref[k : k + 1, :] for k in range(KCONV + 1)]
@@ -446,6 +462,9 @@
 
     def gate(b, sums):
         at = pl.ds(pl.multiple_of(b * rows, rows), rows)
+        for low, t_low in ((b * rows, 0), (b * rows + plan.half, 1)):
+            half_at = pl.ds(pl.multiple_of(low, plan.half), plan.half)
+            got_ref[half_at, :] = jnp.where(t_id == t_low, mine_ref[b], other_ref[b])
         grad_round = got_ref[at, :width]
         factor = got_ref[at, width : width + 128].astype(F32)
         grad_rs = factor[:, 0:1] + factor[:, 2:3]
@@ -678,6 +697,115 @@
     lax.fori_loop(0, width // chunk, weigh, 0)
 
 
+def sum_kernel(plan, got_ref, out_ref):
+    lane = lanes(128)
+    row, count = plan.row, plan.n_small
+    slab = slice(plan.s_dt, plan.s_dt + 128)
+
+    def one(c, _):
+        at = pl.ds(pl.multiple_of(c * plan.d_loc, plan.d_loc), plan.d_loc)
+        total = got_ref[0, at, :].astype(F32)
+        for f in range(1, got_ref.shape[0]):
+            total = total + got_ref[f, at, :].astype(F32)
+        out_ref[at, :] = total.astype(BF)
+        part = total[:, slab]
+        small = part + pltpu.roll(part, 128 - count, 1)
+        high = small.astype(BF).astype(F32)
+        low = pltpu.roll(small - high, count, 1)
+        part = jnp.where(
+            lane < row, part, jnp.where(lane < row + count, high, low)
+        )
+        out_ref[at, slab] = jnp.where(lane < row + 2 * count, part, 0.0).astype(BF)
+        return 0
+
+    lax.fori_loop(0, got_ref.shape[1] // plan.d_loc, one, 0)
+
+
+def pack_kernel(plan, inner_ref, kv_ref, query_ref, dt_ref, bc_ref, gain_ref, conv_ref, chan_ref,
+                mout_ref, aout_ref, out_ref, turn_ref):
+    heads, chan, row = plan.heads, plan.chan, plan.row
+    count = out_ref.shape[0]
+    heads_t, q_t = mout_ref.shape[1] // HDIM, aout_ref.shape[1] // HDIM
+    dts = dt_ref[...].astype(F32)
+    chans = chan_ref[...].astype(F32)
+    query = query_ref[...].astype(F32)
+    turn_ref[...] = jnp.zeros(turn_ref.shape, F32)
+    turn_ref[row : row + 2, : plan.d_loc] = gain_ref[...].astype(F32)
+    turn_ref[row + 2 : row + KCONV + 3, : plan.cc] = conv_ref[...].astype(F32)
+    for c in range(count):
+        live = max(0, min(heads, heads_t - c * heads))
+        wide = live * HDIM
+        out_ref[c] = jnp.zeros(out_ref.shape[1:], BF)
+        out_ref[c, :, : 2 * NSTATE] = bc_ref[...]
+        low = row + KCONV + 3
+        if live:
+            at = c * heads
+            turn_ref[low : low + live, : plan.mc] = chans[at : at + live]
+            turn_ref[plan.off : plan.off + live, : plan.d_loc] = dts[at : at + live]
+        else:
+            turn_ref[low : low + heads, :] = jnp.zeros((heads, 128), F32)
+            turn_ref[plan.off : plan.off + heads, :] = jnp.zeros((heads, 128), F32)
+        slab = turn_ref[...].T[: plan.d_loc]
+        out_ref[c, :, plan.s_dt : plan.s_dt + 128] = slab.astype(BF)
+        if live:
+            at = c * chan
+            out_ref[c, :, plan.o_z : plan.o_z + wide] = inner_ref[:, at : at + wide]
+            at = at + heads_t * HDIM
+            out_ref[c, :, plan.o_x : plan.o_x + wide] = inner_ref[:, at : at + wide]
+            at = c * chan
+            out_ref[c, :, plan.o_mo : plan.o_mo + wide] = mout_ref[:, at : at + wide]
+        if c < q_t:
+            at = c * HDIM
+            out_ref[c, :, plan.o_q : plan.o_q + HDIM] = query[:, at : at + HDIM].astype(BF)
+            out_ref[c, :, plan.o_ao : plan.o_ao + HDIM] = aout_ref[:, at : at + HDIM]
+        out_ref[c, :, plan.o_k : plan.o_k + HDIM] = kv_ref[:, :HDIM]
+        out_ref[c, :, plan.o_v : plan.o_v + HDIM] = kv_ref[:, HDIM:]
+
+
+def unpack_kernel(plan, heads_t, q_t, got_ref, inner_ref, query_ref, dt_ref, kv_ref, mout_ref,
+                  aout_ref, chan_ref, head_ref, tail_ref):
+    heads, chan, off, row = plan.heads, plan.chan, plan.off, plan.row
+    count = got_ref.shape[0]
+    kv_sum = jnp.zeros((plan.d_loc, 128), F32)
+    bc_sum = jnp.zeros((plan.d_loc, 2 * NSTATE), F32)
+    small_sum = jnp.zeros((plan.d_loc, 128), F32)
+    lane = lanes(128)
+    for c in range(count):
+        live = max(0, min(heads, heads_t - c * heads))
+        wide = live * HDIM
+        query = got_ref[c, :, plan.o_q :].astype(F32)[:, :128]
+        value = got_ref[c, :, plan.s_v : plan.s_v + 128].astype(F32)
+        value = value if off == HDIM else pltpu.roll(value, HDIM, 1)
+        kv_sum = kv_sum + jnp.where(lane < HDIM, pltpu.roll(query, HDIM, 1), value)
+        bc_sum = bc_sum + got_ref[c, :, : 2 * NSTATE].astype(F32)
+        slab = got_ref[c, :, plan.s_dt : plan.s_dt + 128].astype(F32)
+        small = slab + pltpu.roll(slab, 128 - plan.n_small, 1)
+        small_sum = small_sum + small
+        if c < q_t:
+            query_ref[:, c * HDIM : (c + 1) * HDIM] = query[:, :HDIM]
+            out = got_ref[c, :, plan.s_ao : plan.s_ao + 128].astype(F32)
+            aout_ref[:, c * HDIM : (c + 1) * HDIM] = out[:, off : off + HDIM]
+        if live:
+            low = c * chan
+            for i, start in enumerate((plan.o_z, plan.o_x)):
+                part = got_ref[c, :, start : start + plan.wide].astype(F32)
+                at = i * heads_t * HDIM + low
+                inner_ref[:, at : at + wide] = part[:, :wide]
+            out = got_ref[c, :, plan.o_mo : plan.o_mo + plan.wide].astype(F32)
+            mout_ref[:, low : low + wide] = out[:, :wide]
+            turned = jnp.where(lane < row, slab, small).T
+            at = c * heads
+            dt_ref[at : at + live, :] = turned[off : off + live, : plan.d_loc]
+            low = row + KCONV + 3
+            chan_ref[at : at + live, :] = turned[low : low + live, : plan.mc]
+            last = turned[row + plan.n_small - 1 : row + plan.n_small]
+            for i in range(3):
+                head_ref[i : i + 1, at : at + live] = last[:, i * heads : i * heads + live]
+    kv_ref[...] = kv_sum
+    tail_ref[:, : 2 * NSTATE] = bc_sum
+    tail_ref[:, 2 * NSTATE :] = small_sum
+
+
 def call(kernel, plan, outs, scratch, scalars, arrays):
     smem = pl.BlockSpec(memory_space=pltpu.SMEM)
     vmem = pl.BlockSpec(memory_space=pltpu.VMEM)
@@ -727,51 +855,28 @@
     cc = bc_conv.shape[1]
     mc = mamba_chan.shape[1]
     plan = Plan(group, rows, width, d_loc, heads, 2 * heads_t * HDIM, cc, mc)
-    chan = plan.chan
     bc_w = 2 * NSTATE
-    o_s, o_end, n_small, p_w = plan.o_s, plan.o_end, plan.n_small, plan.p_w
-
-    def by_context(array, axis, count, size):
-        padded = pad_to(array, axis, count * n_c * size)
-        shape = padded.shape[:axis] + (n_c, count * size) + padded.shape[axis + 1 :]
-        return jnp.moveaxis(padded.reshape(shape), axis, 0)
-
-    inner_ctx = by_context(mamba_in, 2, heads, HDIM)
-    query_ctx = by_context(query_proj, 1, 1, HDIM)
-    dt_ctx = by_context(dt_proj, 1, heads, 1)
-    chan_ctx = pad_to(jnp.swapaxes(by_context(mamba_chan, 0, heads, 1), 1, 2), 1, d_loc)
-    mo_ctx = jnp.swapaxes(by_context(mamba_out, 0, heads, HDIM), 1, 2)
-    ao_ctx = jnp.swapaxes(by_context(attn_out, 0, 1, HDIM), 1, 2)
-
-    def everywhere(array):
-        return jnp.broadcast_to(array[None], (n_c,) + array.shape)
-
-    pieces = [
-        (0, everywhere(bc_proj)),
-        (plan.o_x, inner_ctx[:, :, 1]),
-        (plan.o_v, everywhere(kv_proj[:, 1])),
-        (plan.o_z, inner_ctx[:, :, 0]),
-        (plan.o_dt, dt_ctx),
+    p_w = plan.p_w
+
+    (pack,) = call(
+        pack_kernel,
+        plan,
+        [((n_c, d_loc, p_w), BF)],
+        [((128, 128), F32)],
+        (),
         (
-            plan.o_s,
-            everywhere(jnp.concatenate([norm_gains.T, pad_to(bc_conv.T, 0, d_loc)], axis=1)),
+            mamba_in.reshape(d_loc, 2 * heads_t * HDIM),
+            kv_proj.reshape(d_loc, 2 * HDIM),
+            query_proj,
+            dt_proj.T,
+            bc_proj,
+            norm_gains,
+            bc_conv,
+            mamba_chan,
+            mamba_out.T,
+            attn_out.T,
         ),
-        (plan.o_s + KCONV + 3, chan_ctx),
-        (plan.o_q, query_ctx),
-        (plan.o_k, everywhere(kv_proj[:, 0])),
-        (plan.o_mo, mo_ctx),
-        (plan.o_ao, ao_ctx),
-        (plan.p_w, None),
-    ]
-    columns = []
-    filled = 0
-    for start, piece in pieces:
-        if start > filled:
-            columns.append(jnp.zeros((n_c, d_loc, start - filled), BF))
-        if piece is not None:
-            columns.append(piece)
-            filled = start + piece.shape[2]
-    pack = jnp.concatenate(columns, axis=2)
+    )
 
     mine = lax.dynamic_slice_in_dim(inputs, t_id * half, half, 0)
     part = exchange(pack, "context").reshape(n_c * d_loc, p_w)
@@ -789,8 +894,7 @@
     positions = row_ids - jnp.max(jnp.where(inside, starts[None, :], 0), axis=1)
     freqs = jnp.power(ROPE_BASE, -jnp.arange(HDIM // 2).astype(F32) * (2.0 / HDIM))
     angles = positions.astype(F32)[:, None] * jnp.concatenate([freqs] * 4)[None, :]
-    cosine = jnp.cos(angles)
-    sine = jnp.sin(angles)
+    trig = jnp.concatenate([jnp.cos(angles), jnp.sin(angles)], axis=1)
     head_vec = lax.dynamic_slice_in_dim(
         pad_to(head_params, 1, heads_pad), c_id * heads, heads, 1
     )
@@ -805,27 +909,24 @@
     scalars = (seq_lengths, head_vec, t_id.reshape(1))
     slab_w = 2 * width + 128
     part_rows = n_c * half
-    keep, give, gain_two, taps, norm, proj, pre, cum, ssm, attn, lse, qk, kq = call(
+    keep, give, gain_one, gain_two, taps, norm, proj, pre, wide, thin = call(
         forward_kernel,
         plan,
         [
             ((part_rows, slab_w), BF),
             ((part_rows, slab_w), BF),
             ((1, width), F32),
+            ((1, width), F32),
             ((8, plan.conv), F32),
             ((group, width), BF),
             ((group, plan.a_w), F32),
             ((group, plan.conv), F32),
-            ((group, 128), F32),
-            ((group, plan.wide), F32),
-            ((group, 128), BF),
-            ((group, 128), F32),
-            ((group, 128), BF),
-            ((group, 128), BF),
+            ((group, plan.wide + 256), F32),
+            ((group, 384), BF),
         ],
         [((group, plan.conv), BF), ((group + 8, plan.conv), F32), ((group, 128), F32)],
         scalars,
-        (rows_in, w_all, sel, cosine, sine),
+        (rows_in, w_all, sel, trig),
     )
     gain_mlp = gain_two[0]
 
@@ -877,7 +978,7 @@
     grad_rs_own = jnp.sum(grad_res * mamba_own, axis=1, keepdims=True)
     factor = split(jnp.concatenate([grad_rs_own, scale_own], axis=1), 2)
     got = spread(jnp.concatenate([grad_res.astype(BF), factor], axis=1), "context")
-    got = join_pair(got, swap_pair(got), t_id, 1).reshape(group, -1)
+    got_other = swap_pair(got)
     block = n_c * d_loc
 
     def mlp_block(target, part):
@@ -912,10 +1013,12 @@
             ((128, group), F32),
             ((width, 128), F32),
             ((group, 128), F32),
+            ((group, width + 128), BF),
         ],
         scalars,
         (
-            rows_in, w_all, sel, cosine, sine, taps, norm, proj, pre, cum, ssm, attn, lse, qk, kq, got,
+            rows_in, w_all, sel, trig, taps, norm, proj, pre, wide, thin, got,
+            got_other,
             g_gain_mlp[None],
         ),
     )
@@ -923,53 +1026,41 @@
     out_own = (residual + pair_sum(dot_nt(mlp_act, w_mo), ())).astype(BF)
     partial = pair_add(keep, give).reshape(n_c, half, width)
     grad_one = reduce_async(partial, "context")
-    gain_mix = w_all[:, o_s].astype(F32)
+    gain_mix = gain_one[0]
     normed_own, inv_own = rms_forward(in_own)
     grad_in_own = grad_res + rms_backward(grad_one, normed_own, inv_own, gain_mix)
     output = join_pair(out_own, swap_pair(out_own), t_id, 0).reshape(rows, width)
     input_grad = join_pair(grad_in_own, swap_pair(grad_in_own), t_id, 0).reshape(rows, width)
 
     got = exchange(g_pack.reshape(n_f, block, p_w), "fsdp")
-    got = jnp.sum(got.astype(F32), axis=0)
-    g_small = fuse(got[:, o_s:o_end], 2, n_small)
-    g_pack = jnp.concatenate(
-        [got[:, :o_s].astype(BF), split(g_small, 2, False), got[:, o_end:].astype(BF)], axis=1
-    )
-    g_a = exchange(g_pack.reshape(n_c, d_loc, p_w), "context").astype(F32)
-
-    def joined(low, size, count):
-        moved = jnp.moveaxis(g_a[:, :, low : low + size], 0, 1).reshape(d_loc, n_c * size)
-        return moved[:, : count]
-
-    out_inner = jnp.stack(
+    (g_pack,) = call(sum_kernel, plan, [((block, p_w), BF)], [], (), (got,))
+    got = exchange(g_pack.reshape(n_c, d_loc, p_w), "context")
+    out_inner, out_query, out_dt, out_kv, out_mout, out_aout, out_chan, out_heads, tail = call(
+        lambda plan, *refs: unpack_kernel(plan, heads_t, q_t, *refs),
+        plan,
         [
-            joined(plan.o_z, chan, heads_t * HDIM),
-            joined(plan.o_x, chan, heads_t * HDIM),
+            ((d_loc, 2 * heads_t * HDIM), F32),
+            ((d_loc, q_t * HDIM), F32),
+            ((heads_t, d_loc), F32),
+            ((d_loc, 2 * HDIM), F32),
+            ((d_loc, heads_t * HDIM), F32),
+            ((d_loc, q_t * HDIM), F32),
+            ((heads_t, mc), F32),
+            ((3, heads_t), F32),
+            ((d_loc, bc_w + 128), F32),
         ],
-        axis=1,
-    )
-    out_query = joined(plan.o_q, HDIM, q_t * HDIM)
-    out_dt = joined(plan.o_dt, heads, heads_t)
-    out_kv = jnp.stack(
-        [
-            jnp.sum(g_a[:, :, plan.o_k : plan.o_k + HDIM], axis=0),
-            jnp.sum(g_a[:, :, plan.o_v : plan.o_v + HDIM], axis=0),
-        ],
-        axis=1,
-    )
-    out_mout = joined(plan.o_mo, chan, heads_t * HDIM).T
-    out_aout = joined(plan.o_ao, HDIM, q_t * HDIM).T
-    g_small = fuse(g_a[:, :, o_s:o_end], 2, n_small)
-    tail = jnp.concatenate([g_a[:, :, :bc_w], g_small[:, :, : KCONV + 3]], axis=2)
-    tail = jnp.sum(tail, axis=0)
+        [],
+        (),
+        (got,),
+    )
     tail = tail + swap_pair(tail)
+    out_inner = out_inner.reshape(d_loc, 2, heads_t * HDIM)
+    out_kv = out_kv.reshape(d_loc, 2, HDIM)
+    out_dt, out_mout, out_aout = out_dt.T, out_mout.T, out_aout.T
     out_bc = tail[:, :bc_w]
-    out_gains = tail[:, bc_w : bc_w + 2].T
-    out_convbc = tail[:cc, bc_w + 2 :].T
-    out_chan = jnp.swapaxes(g_small[:, :mc, KCONV + 3 : KCONV + 3 + heads], 1, 2)
-    out_chan = out_chan.reshape(heads_pad, mc)[:heads_t]
-    out_heads = g_small[:, : 3 * heads, n_small - 1].reshape(n_c, 3, heads)
-    out_heads = jnp.swapaxes(out_heads, 0, 1).reshape(3, heads_pad)[:, :heads_t]
+    low = bc_w + plan.row
+    out_gains = tail[:, low : low + 2].T
+    out_convbc = tail[:cc, low + 2 : low + KCONV + 3].T
 
     return (
         output,

time: 340 us -> 330 us (0.971)
  local copies, waits for them, and re-layouts: 54.9 us -> 45.1 us
  other arithmetic: 35.2 us -> 28.3 us
  Pallas kernels: 37.1 us -> 41.3 us
    reshape x12 -> x3, local copies, waits for them, and re-layouts: 9.67 us -> 2.58 us  [the longest x1 1.01 us: per_device(): out_inner = out_inner.reshape(d_loc, 2, heads_t * HDIM)]
    unnamed x109 -> x104, local copies, waits for them, and re-layouts: 5.8 us -> 11.3 us
    pallas_call x2 -> x5, Pallas kernels: 37.1 us -> 41.3 us  [call(): pl.pallas_call(lambda *refs: kernel(plan, *refs), out_shape=[jax.ShapeDty...]
  transfers between devices with their start and end apart: 45 -> 45, of which waited for: 14 -> 14; matrix products, arithmetic and copies ran while one was open for 28% -> 24% of each run, Pallas kernels for 4% -> 5%
where the time goes in v1:
time: 330 us; the launch traced here: 328 us
  waiting for transfers between devices  121 us (37%)
  starting transfers between devices  65.2 us (20%)
  local copies, waits for them, and re-layouts  45.1 us (14%)
  Pallas kernels  41.3 us (13%)
  other arithmetic  28.3 us (9%)
  matrix products  25.5 us (8%)
    pallas_call x5, Pallas kernels, call(): pl.pallas_call(lambda *refs: kernel(plan, *refs), out_shape=[jax.ShapeDty...  41.3 us
    ppermute x6, waiting for transfers between devices, reduce_async(): lax.ppermute(lax.dynamic_index_in_dim(blocks, target, 0, False), axis, ro...  32.7 us
    all_to_all x6, waiting for transfers between devices, exchange(): return lax.all_to_all(blocks, axis, 0, 0, tiled=True)  31.4 us
    all_to_all x6, starting transfers between devices, exchange(): return lax.all_to_all(blocks, axis, 0, 0, tiled=True)  24.2 us
    ppermute x2, waiting for transfers between devices, plane_gather(): far_top = lax.ppermute(side[:half], 'fsdp', beside(1))  20.3 us
    ppermute x9, starting transfers between devices, spread_async(): lax.ppermute(block, axis, route)  16.6 us
    dot_general x8, matrix products, dot_tn(): lax.dot_general(left, right, (((0,), (0,)), ((), ())), precision=exact, p...  15.3 us
    dynamic_update_slice x6, local copies, waits for them, and re-layouts, plane_gather(): whole = lax.dynamic_update_slice(whole, piece, (index, 0, 0, 0))  12.3 us
  transfers between devices with their start and end apart: 45, of which 14 were waited for; matrix products, arithmetic and copies ran while one was open for 24% of the time, Pallas kernels for 5%

profile of v1, /device:TPU:0, one launch (start us, length us, event | category | flops | bytes accessed | tf_op | source)
XLA Modules:
  0.0 328.2 jit_solution(9674787500708004218)
XLA Ops:
  1.8 5.1 %collective-permute-start.2 = (bf16[64,1024]{1,0:T(8,128)(2,1)S(1)}, bf16[64,1024]{1,0:T(8,128)(2,1)S(1)}, u32[]{:S(2)}, u32[]{:S(2)}) collective-permute-start(bf16[64,1024]{1,0:T(8,128)(2,1)S(1)} %get-tuple-element.113), channel_id=1, source_target_pairs={{0,6},{2,0},{4,2},{6,4},{1,7},{3,1},{5,3},{7,5},{8,14},{10,8},{12,... | collective-permute-start | bytes 393224 | tf_op jit(solution)/shard_map/ppermute | solution.py:47
  21.5 3.5 %all-to-all-start = ((bf16[4,64,1152]{2,1,0:T(8,128)(2,1)}), bf16[4,64,1152]{2,1,0:T(8,128)(2,1)S(1)}, u32[]{:S(2)}, u32[]{:S(2)}) async-start(bf16[4,64,1152]{2,1,0:T(8,128)(2,1)} %shard_map.271), calls=%async_computation | async-start | bytes 1179648 | tf_op jit(solution)/shard_map/all_to_all | solution.py:30
  29.5 10.2 %all-to-all-done = bf16[4,64,1152]{2,1,0:T(8,128)(2,1)S(1)} async-done(((bf16[4,64,1152]{2,1,0:T(8,128)(2,1)}), bf16[4,64,1152]{2,1,0:T(8,128)(2,1)S(1)}, u32[]{:S(2)}, u32[]{:S(2)}) %all-to-all-start) | async-done | bytes 589856 | tf_op jit(solution)/shard_map/all_to_all | solution.py:30
  41.3 4.6 %all-to-all-start.1 = ((bf16[4,256,1152]{2,1,0:T(8,128)(2,1)}), bf16[4,256,1152]{2,1,0:T(8,128)(2,1)}, u32[]{:S(2)}, u32[]{:S(2)}) async-start(bf16[4,256,1152]{2,1,0:T(8,128)(2,1)} %broadcast_in_dim.35), calls=%async_computation.1 | async-start | bytes 4718592 | tf_op jit(solution)/shard_map/all_to_all | solution.py:30
  47.2 3.6 %collective-permute-start.8 = (bf16[64,2048]{1,0:T(8,128)(2,1)S(1)}, bf16[64,2048]{1,0:T(8,128)(2,1)}, u32[]{:S(2)}, u32[]{:S(2)}) collective-permute-start(bf16[64,2048]{1,0:T(8,128)(2,1)S(1)} %bitcast.181), channel_id=1, source_target_pairs={{0,6},{2,0},{4,2},{6,4},{1,7},{3,1},{5,3},{7,5},{8,14},{10,8},{12,... | collective-permute-start | bytes 786440 | tf_op jit(solution)/shard_map/ppermute | solution.py:47
  62.5 11.7 %all-to-all-done.1 = bf16[4,256,1152]{2,1,0:T(8,128)(2,1)} async-done(((bf16[4,256,1152]{2,1,0:T(8,128)(2,1)}), bf16[4,256,1152]{2,1,0:T(8,128)(2,1)}, u32[]{:S(2)}, u32[]{:S(2)}) %all-to-all-start.1) | async-done | bytes 2359328 | tf_op jit(solution)/shard_map/all_to_all | solution.py:30
  74.2 14.5 %shard_map.272 = (bf16[256,2176]{1,0:T(8,128)(2,1)}, bf16[256,2176]{1,0:T(8,128)(2,1)}, f32[1,1024]{1,0:T(1,128)S(1)}, f32[1,1024]{1,0:T(1,128)S(1)}, f32[8,512]...) custom-call(s32[1,2]{1,0:T(1,128)S(1)} %copy-done.14, ...), custom_call_target="tpu_custom_call" | custom-call | tf_op jit(solution)/shard_map/pallas_call | solution.py:812
  109.0 4.5 %all-to-all-start.2 = ((bf16[4,64,2176]{2,1,0:T(8,128)(2,1)}), bf16[4,64,2176]{2,1,0:T(8,128)(2,1)}, u32[]{:S(2)}, u32[]{:S(2)}) async-start(bf16[4,64,2176]{2,1,0:T(8,128)(2,1)} %bitcast.173), calls=%async_computation.2 | async-start | bytes 2228224 | tf_op jit(solution)/shard_map/all_to_all | solution.py:30
  117.2 15.6 %collective-permute-done.18 = bf16[128,1024]{1,0:T(8,128)(2,1)S(1)} collective-permute-done((bf16[128,1024]{1,0:T(8,128)(2,1)}, bf16[128,1024]{1,0:T(8,128)(2,1)S(1)}, u32[]{:S(2)}, u32[]{:S(2)}) %collective-permute-start.18) | collective-permute-done | bytes 262176 | tf_op jit(solution)/shard_map/ppermute | solution.py:83
  143.1 4.7 %collective-permute-done.11 = bf16[128,2048]{1,0:T(8,128)(2,1)S(1)} collective-permute-done((bf16[128,2048]{1,0:T(8,128)(2,1)S(1)}, bf16[128,2048]{1,0:T(8,128)(2,1)S(1)}, u32[]{:S(2)}, u32[]{:S(2)}) %collective-permute-start.11) | collective-permute-done | bytes 524320 | tf_op jit(solution)/shard_map/ppermute | solution.py:83
  156.9 3.9 %fusion.90 = f32[2,64,1024]{2,1,0:T(8,128)S(1)} fusion(bf16[2,64,2048]{2,1,0:T(8,128)(2,1)S(1)} %bitcast.179, bf16[1024,2048,1]{1,0,2:T(8,128)(2,1)} %bitcast.44), kind=kOutput, calls=%fused_computation.208 | convolution fusion | flops 536870912 | bytes 5242880 | tf_op jit(solution)/shard_map/dot_general | solution.py:148
  169.7 4.4 %all-to-all-start.3 = ((bf16[4,64,1152]{2,1,0:T(8,128)(2,1)}), bf16[4,64,1152]{2,1,0:T(8,128)(2,1)S(1)}, u32[]{:S(2)}, u32[]{:S(2)}) async-start(bf16[4,64,1152]{2,1,0:T(8,128)(2,1)} %broadcast_in_dim.73), calls=%async_computation.3 | async-start | bytes 1179648 | tf_op jit(solution)/shard_map/all_to_all | solution.py:30
  174.1 10.9 %collective-permute-done.31 = bf16[128,3072]{1,0:T(8,128)(2,1)} collective-permute-done((bf16[128,3072]{1,0:T(8,128)(2,1)}, bf16[128,3072]{1,0:T(8,128)(2,1)}, u32[]{:S(2)}, u32[]{:S(2)}) %collective-permute-start.31) | collective-permute-done | bytes 786464 | tf_op jit(solution)/shard_map/ppermute | solution.py:106
  198.0 3.8 %collective-permute-done.30 = bf16[128,3072]{1,0:T(8,128)(2,1)} collective-permute-done((bf16[128,3072]{1,0:T(8,128)(2,1)}, bf16[128,3072]{1,0:T(8,128)(2,1)}, u32[]{:S(2)}, u32[]{:S(2)}) %collective-permute-start.30) | collective-permute-done | bytes 786464 | tf_op jit(solution)/shard_map/ppermute | solution.py:108
  201.8 6.7 %collective-permute-done.32 = bf16[128,3072]{1,0:T(8,128)(2,1)} collective-permute-done((bf16[128,3072]{1,0:T(8,128)(2,1)}, bf16[128,3072]{1,0:T(8,128)(2,1)}, u32[]{:S(2)}, u32[]{:S(2)}) %collective-permute-start.32) | collective-permute-done | bytes 786464 | tf_op jit(solution)/shard_map/ppermute | solution.py:116
  210.6 12.2 %collective-permute-done.35 = bf16[128,3072]{1,0:T(8,128)(2,1)} collective-permute-done((bf16[128,3072]{1,0:T(8,128)(2,1)}, bf16[128,3072]{1,0:T(8,128)(2,1)}, u32[]{:S(2)}, u32[]{:S(2)}) %collective-permute-start.35) | collective-permute-done | bytes 786464 | tf_op jit(solution)/shard_map/ppermute | solution.py:109
  226.1 23.2 %shard_map.273 = (bf16[256,1024]{1,0:T(8,128)(2,1)S(1)}, bf16[256,1024]{1,0:T(8,128)(2,1)S(1)}, bf16[1024,1152]{1,0:T(8,128)(2,1)}) custom-call(s32[1,2]{1,0:T(1,128)S(1)} %copy-done.14, f32[3,3]{1,0:T(4,128)S(1)} %constant_dynamic-slice_fusion.refs_1_, s32[1]{0:T(128)} %bitcast.refs_2_, bf16[512,1024]{1,0:T(8,128)(2,1)S(1)} %bitcast.157, ...), custom_call_target="tpu_custom_call" | custom-call | tf_op jit(solution)/shard_map/pallas_call | solution.py:812
  250.9 3.8 %all-to-all-start.4 = ((bf16[4,256,1152]{2,1,0:T(8,128)(2,1)}), bf16[4,256,1152]{2,1,0:T(8,128)(2,1)S(1)}, u32[]{:S(2)}, u32[]{:S(2)}) async-start(bf16[4,256,1152]{2,1,0:T(8,128)(2,1)} %bitcast.177), calls=%async_computation.4 | async-start | bytes 4718592 | tf_op jit(solution)/shard_map/all_to_all | solution.py:30
  259.5 3.3 collective-permute-start.38
  263.2 3.8 %collective-permute-start.27 = (bf16[64,1024]{1,0:T(8,128)(2,1)S(1)}, bf16[64,1024]{1,0:T(8,128)(2,1)S(1)}, u32[]{:S(2)}, u32[]{:S(2)}) collective-permute-start(bf16[64,1024]{1,0:T(8,128)(2,1)S(1)} %get-tuple-element.133), channel_id=1, source_target_pairs={{0,6},{2,0},{4,2},{6,4},{1,7},{3,1},{5,3},{7,5},{8,14},{10,8},{12,... | collective-permute-start | bytes 393224 | tf_op jit(solution)/shard_map/ppermute | solution.py:63
  267.8 16.4 %collective-permute-done.25 = bf16[64,1024]{1,0:T(8,128)(2,1)S(1)} collective-permute-done((bf16[64,1024]{1,0:T(8,128)(2,1)S(1)}, bf16[64,1024]{1,0:T(8,128)(2,1)S(1)}, u32[]{:S(2)}, u32[]{:S(2)}) %collective-permute-start.25) | collective-permute-done | bytes 131104 | tf_op jit(solution)/shard_map/ppermute | solution.py:63
  286.8 13.4 %collective-permute-done.26 = bf16[64,1024]{1,0:T(8,128)(2,1)S(1)} collective-permute-done((bf16[64,1024]{1,0:T(8,128)(2,1)S(1)}, bf16[64,1024]{1,0:T(8,128)(2,1)S(1)}, u32[]{:S(2)}, u32[]{:S(2)}) %collective-permute-start.26) | collective-permute-done | bytes 131104 | tf_op jit(solution)/shard_map/ppermute | solution.py:63
  302.2 3.5 %all-to-all-start.5 = ((bf16[4,64,1152]{2,1,0:T(8,128)(2,1)}), bf16[4,64,1152]{2,1,0:T(8,128)(2,1)S(1)}, u32[]{:S(2)}, u32[]{:S(2)}) async-start(bf16[4,64,1152]{2,1,0:T(8,128)(2,1)} %bitcast.67), calls=%async_computation.5 | async-start | bytes 1179648 | tf_op jit(solution)/shard_map/all_to_all | solution.py:30
  313.0 9.4 %all-to-all-done.5.refs_0_ = bf16[4,64,1152]{2,1,0:T(8,128)(2,1)S(1)} async-done(((bf16[4,64,1152]{2,1,0:T(8,128)(2,1)}), bf16[4,64,1152]{2,1,0:T(8,128)(2,1)S(1)}, u32[]{:S(2)}, u32[]{:S(2)}) %all-to-all-start.5) | async-done | bytes 589856 | tf_op jit(solution)/shard_map/all_to_all | solution.py:30
  (283 shorter events, 129.8 us)
Async XLA Ops:
  1.8 45.1 %collective-permute-start.2 = (bf16[64,1024]{1,0:T(8,128)(2,1)S(1)}, bf16[64,1024]{1,0:T(8,128)(2,1)S(1)}, u32[]{:S(2)}, u32[]{:S(2)}) collective-permute-start(bf16[64,1024]{1,0:T(8,128)(2,1)S(1)} %get-tuple-element.113), channel_id=1, source_target_pairs={{0,6},{2,0},{4,2},{6,4},{1,7},{3,1},{5,3},{7,5},{8,14},{10,8},{12,... | collective-permute-start | bytes 393224 | tf_op jit(solution)/shard_map/ppermute | solution.py:47
  6.9 40.3 %collective-permute-start.1 = (bf16[64,1024]{1,0:T(8,128)(2,1)S(1)}, bf16[64,1024]{1,0:T(8,128)(2,1)}, u32[]{:S(2)}, u32[]{:S(2)}) collective-permute-start(bf16[64,1024]{1,0:T(8,128)(2,1)S(1)} %get-tuple-element.113), channel_id=1, source_target_pairs={{0,4},{2,6},{4,0},{6,2},{1,5},{3,7},{5,1},{7,3},{8,12},{10,14},{12... | collective-permute-start | bytes 393224 | tf_op jit(solution)/shard_map/ppermute | solution.py:47
  6.9 43.8 %collective-permute-start = (bf16[64,1024]{1,0:T(8,128)(2,1)S(1)}, bf16[64,1024]{1,0:T(8,128)(2,1)}, u32[]{:S(2)}, u32[]{:S(2)}) collective-permute-start(bf16[64,1024]{1,0:T(8,128)(2,1)S(1)} %get-tuple-element.113), channel_id=1, source_target_pairs={{0,2},{2,4},{4,6},{6,0},{1,3},{3,5},{5,7},{7,1},{8,10},{10,12},{12... | collective-permute-start | bytes 393224 | tf_op jit(solution)/shard_map/ppermute | solution.py:47
  7.9 47.5 %collective-permute-start.14 = (bf16[64,1024]{1,0:T(8,128)(2,1)}, bf16[64,1024]{1,0:T(8,128)(2,1)}, u32[]{:S(2)}, u32[]{:S(2)}) collective-permute-start(bf16[64,1024]{1,0:T(8,128)(2,1)} %bitcast.199), channel_id=1, source_target_pairs={{0,4},{2,6},{4,0},{6,2},{1,5},{3,7},{5,1},{7,3},{8,12},{10,14},{12... | collective-permute-start | bytes 393224 | tf_op jit(solution)/shard_map/ppermute | solution.py:47
  9.8 45.7 %collective-permute-start.15 = (bf16[64,1024]{1,0:T(8,128)(2,1)}, bf16[64,1024]{1,0:T(8,128)(2,1)}, u32[]{:S(2)}, u32[]{:S(2)}) collective-permute-start(bf16[64,1024]{1,0:T(8,128)(2,1)} %bitcast.200), channel_id=1, source_target_pairs={{0,6},{2,0},{4,2},{6,4},{1,7},{3,1},{5,3},{7,5},{8,14},{10,8},{12,... | collective-permute-start | bytes 393224 | tf_op jit(solution)/shard_map/ppermute | solution.py:47
  41.3 32.9 %all-to-all-start.1 = ((bf16[4,256,1152]{2,1,0:T(8,128)(2,1)}), bf16[4,256,1152]{2,1,0:T(8,128)(2,1)}, u32[]{:S(2)}, u32[]{:S(2)}) async-start(bf16[4,256,1152]{2,1,0:T(8,128)(2,1)} %broadcast_in_dim.35), calls=%async_computation.1 | async-start | bytes 4718592 | tf_op jit(solution)/shard_map/all_to_all | solution.py:30
  47.2 43.4 %collective-permute-start.8 = (bf16[64,2048]{1,0:T(8,128)(2,1)S(1)}, bf16[64,2048]{1,0:T(8,128)(2,1)}, u32[]{:S(2)}, u32[]{:S(2)}) collective-permute-start(bf16[64,2048]{1,0:T(8,128)(2,1)S(1)} %bitcast.181), channel_id=1, source_target_pairs={{0,6},{2,0},{4,2},{6,4},{1,7},{3,1},{5,3},{7,5},{8,14},{10,8},{12,... | collective-permute-start | bytes 786440 | tf_op jit(solution)/shard_map/ppermute | solution.py:47
  55.4 35.8 %collective-permute-start.7 = (bf16[64,2048]{1,0:T(8,128)(2,1)S(1)}, bf16[64,2048]{1,0:T(8,128)(2,1)S(1)}, u32[]{:S(2)}, u32[]{:S(2)}) collective-permute-start(bf16[64,2048]{1,0:T(8,128)(2,1)S(1)} %bitcast.182), channel_id=1, source_target_pairs={{0,4},{2,6},{4,0},{6,2},{1,5},{3,7},{5,1},{7,3},{8,12},{10,14},{12... | collective-permute-start | bytes 786440 | tf_op jit(solution)/shard_map/ppermute | solution.py:47
  55.5 35.7 %collective-permute-start.6 = (bf16[64,2048]{1,0:T(8,128)(2,1)S(1)}, bf16[64,2048]{1,0:T(8,128)(2,1)}, u32[]{:S(2)}, u32[]{:S(2)}) collective-permute-start(bf16[64,2048]{1,0:T(8,128)(2,1)S(1)} %bitcast.183), channel_id=1, source_target_pairs={{0,2},{2,4},{4,6},{6,0},{1,3},{3,5},{5,7},{7,1},{8,10},{10,12},{12... | collective-permute-start | bytes 786440 | tf_op jit(solution)/shard_map/ppermute | solution.py:47
  59.2 41.3 %collective-permute-start.17 = (bf16[256,1024]{1,0:T(8,128)(2,1)}, bf16[256,1024]{1,0:T(8,128)(2,1)}, u32[]{:S(2)}, u32[]{:S(2)}) collective-permute-start(bf16[256,1024]{1,0:T(8,128)(2,1)} %bitcast.36), channel_id=1, source_target_pairs={{0,16},{8,24},{16,0},{24,8},{1,17},{9,25},{17,1},{25,9},{2,18},{10... | collective-permute-start | bytes 1572872 | tf_op jit(solution)/shard_map/ppermute | solution.py:82
  93.5 40.0 %collective-permute-start.10 = (bf16[256,2048]{1,0:T(8,128)(2,1)}, bf16[256,2048]{1,0:T(8,128)(2,1)}, u32[]{:S(2)}, u32[]{:S(2)}) collective-permute-start(bf16[256,2048]{1,0:T(8,128)(2,1)} %bitcast.24), channel_id=1, source_target_pairs={{0,16},{8,24},{16,0},{24,8},{1,17},{9,25},{17,1},{25,9},{2,18},{10... | collective-permute-start | bytes 3145736 | tf_op jit(solution)/shard_map/ppermute | solution.py:82
  94.1 41.9 %collective-permute-start.9 = (bf16[256,2048]{1,0:T(8,128)(2,1)}, bf16[256,2048]{1,0:T(8,128)(2,1)}, u32[]{:S(2)}, u32[]{:S(2)}) collective-permute-start(bf16[256,2048]{1,0:T(8,128)(2,1)} %bitcast.24), channel_id=1, source_target_pairs={{0,8},{8,0},{16,24},{24,16},{1,9},{9,1},{17,25},{25,17},{2,10},{10... | collective-permute-start | bytes 3145736 | tf_op jit(solution)/shard_map/ppermute | solution.py:81
  102.1 30.7 %collective-permute-start.18 = (bf16[128,1024]{1,0:T(8,128)(2,1)}, bf16[128,1024]{1,0:T(8,128)(2,1)S(1)}, u32[]{:S(2)}, u32[]{:S(2)}) collective-permute-start(bf16[128,1024]{1,0:T(8,128)(2,1)} %slice.65), channel_id=1, source_target_pairs={{0,8},{8,0},{16,24},{24,16},{1,9},{9,1},{17,25},{25,17},{2,10},{10... | collective-permute-start | bytes 786440 | tf_op jit(solution)/shard_map/ppermute | solution.py:83
  107.1 28.2 %collective-permute-start.19 = (bf16[128,1024]{1,0:T(8,128)(2,1)}, bf16[128,1024]{1,0:T(8,128)(2,1)S(1)}, u32[]{:S(2)}, u32[]{:S(2)}) collective-permute-start(bf16[128,1024]{1,0:T(8,128)(2,1)} %slice.66), channel_id=1, source_target_pairs={{0,16},{8,24},{16,0},{24,8},{1,17},{9,25},{17,1},{25,9},{2,18},{10... | collective-permute-start | bytes 786440 | tf_op jit(solution)/shard_map/ppermute | solution.py:84
  109.0 39.7 %all-to-all-start.2 = ((bf16[4,64,2176]{2,1,0:T(8,128)(2,1)}), bf16[4,64,2176]{2,1,0:T(8,128)(2,1)}, u32[]{:S(2)}, u32[]{:S(2)}) async-start(bf16[4,64,2176]{2,1,0:T(8,128)(2,1)} %bitcast.173), calls=%async_computation.2 | async-start | bytes 2228224 | tf_op jit(solution)/shard_map/all_to_all | solution.py:30
  163.7 28.8 %collective-permute-start.33 = (bf16[128,3072]{1,0:T(8,128)(2,1)}, bf16[128,3072]{1,0:T(8,128)(2,1)}, u32[]{:S(2)}, u32[]{:S(2)}) collective-permute-start(bf16[128,3072]{1,0:T(8,128)(2,1)} %convolution_convert_fusion.1), channel_id=1, source_target_pairs={{0,16},{8,24},{16,0},{24,8},{1,17},{9,25},{17,1},{25,9},{2,18},{10... | collective-permute-start | bytes 2359304 | tf_op jit(solution)/shard_map/ppermute | solution.py:107
  166.9 34.9 %collective-permute-start.30 = (bf16[128,3072]{1,0:T(8,128)(2,1)}, bf16[128,3072]{1,0:T(8,128)(2,1)}, u32[]{:S(2)}, u32[]{:S(2)}) collective-permute-start(bf16[128,3072]{1,0:T(8,128)(2,1)} %convolution_convert_fusion.6), channel_id=1, source_target_pairs={{0,8},{8,0},{16,24},{24,16},{1,9},{9,1},{17,25},{25,17},{2,10},{10... | collective-permute-start | bytes 2359304 | tf_op jit(solution)/shard_map/ppermute | solution.py:108
  169.7 28.2 %all-to-all-start.3 = ((bf16[4,64,1152]{2,1,0:T(8,128)(2,1)}), bf16[4,64,1152]{2,1,0:T(8,128)(2,1)S(1)}, u32[]{:S(2)}, u32[]{:S(2)}) async-start(bf16[4,64,1152]{2,1,0:T(8,128)(2,1)} %broadcast_in_dim.73), calls=%async_computation.3 | async-start | bytes 1179648 | tf_op jit(solution)/shard_map/all_to_all | solution.py:30
  191.9 30.9 %collective-permute-start.35 = (bf16[128,3072]{1,0:T(8,128)(2,1)}, bf16[128,3072]{1,0:T(8,128)(2,1)}, u32[]{:S(2)}, u32[]{:S(2)}) collective-permute-start(bf16[128,3072]{1,0:T(8,128)(2,1)} %convolution_convert_fusion), channel_id=1, source_target_pairs={{0,16},{8,24},{16,0},{24,8},{1,17},{9,25},{17,1},{25,9},{2,18},{10... | collective-permute-start | bytes 2359304 | tf_op jit(solution)/shard_map/ppermute | solution.py:109
  197.9 28.2 %collective-permute-start.21 = (bf16[4,64,1152]{2,1,0:T(8,128)(2,1)S(1)}, bf16[4,64,1152]{2,1,0:T(8,128)(2,1)S(1)}, u32[]{:S(2)}, u32[]{:S(2)}) collective-permute-start(bf16[4,64,1152]{2,1,0:T(8,128)(2,1)S(1)} %all-to-all-done.3.refs_13_), channel_id=1, source_target_pairs={{0,1},{1,0},{2,3},{3,2},{4,5},{5,4},{6,7},{7,6},{8,9},{9,8},{10,11... | collective-permute-start | bytes 1769480 | tf_op jit(solution)/shard_map/ppermute | solution.py:20
  250.9 49.8 %all-to-all-start.4 = ((bf16[4,256,1152]{2,1,0:T(8,128)(2,1)}), bf16[4,256,1152]{2,1,0:T(8,128)(2,1)S(1)}, u32[]{:S(2)}, u32[]{:S(2)}) async-start(bf16[4,256,1152]{2,1,0:T(8,128)(2,1)} %bitcast.177), calls=%async_computation.4 | async-start | bytes 4718592 | tf_op jit(solution)/shard_map/all_to_all | solution.py:30
  258.9 46.7 %collective-permute-start.36 = (bf16[64,3072]{1,0:T(8,128)(2,1)}, bf16[64,3072]{1,0:T(8,128)(2,1)S(1)}, u32[]{:S(2)}, u32[]{:S(2)}) collective-permute-start(bf16[64,3072]{1,0:T(8,128)(2,1)} %get-tuple-element.118), channel_id=1, source_target_pairs={{0,2},{2,4},{4,6},{6,0},{1,3},{3,5},{5,7},{7,1},{8,10},{10,12},{12... | collective-permute-start | bytes 1179656 | tf_op jit(solution)/shard_map/ppermute | solution.py:63
  259.5 46.2 %collective-permute-start.38 = (bf16[64,3072]{1,0:T(8,128)(2,1)}, bf16[64,3072]{1,0:T(8,128)(2,1)}, u32[]{:S(2)}, u32[]{:S(2)}) collective-permute-start(bf16[64,3072]{1,0:T(8,128)(2,1)} %get-tuple-element.119), channel_id=1, source_target_pairs={{0,6},{2,0},{4,2},{6,4},{1,7},{3,1},{5,3},{7,5},{8,14},{10,8},{12,... | collective-permute-start | bytes 1179656 | tf_op jit(solution)/shard_map/ppermute | solution.py:63
  267.0 33.2 %collective-permute-start.26 = (bf16[64,1024]{1,0:T(8,128)(2,1)S(1)}, bf16[64,1024]{1,0:T(8,128)(2,1)S(1)}, u32[]{:S(2)}, u32[]{:S(2)}) collective-permute-start(bf16[64,1024]{1,0:T(8,128)(2,1)S(1)} %get-tuple-element.134), channel_id=1, source_target_pairs={{0,4},{2,6},{4,0},{6,2},{1,5},{3,7},{5,1},{7,3},{8,12},{10,14},{12... | collective-permute-start | bytes 393224 | tf_op jit(solution)/shard_map/ppermute | solution.py:63
  (71 other events, 915.2 us)

commit v2 on v1

--- a/solution.py
+++ b/solution.py
@@ -4,6 +4,10 @@
 from jax.experimental import pallas as pl
 from jax.experimental.pallas import tpu as pltpu
 from jax.sharding import PartitionSpec as P
+
+S_TENSOR = "tensor"
+S_FSDP = "fsdp"
+S_CONTEXT = "context"
 
 
 HDIM = 64
@@ -17,7 +21,7 @@
 
 
 def swap_pair(block):
-    return lax.ppermute(block, "tensor", [(0, 1), (1, 0)])
+    return lax.ppermute(block, S_TENSOR, [(0, 1), (1, 0)])
 
 
 def join_pair(own, other, place, axis):
@@ -74,14 +78,14 @@
 
 
 def plane_gather(block):
-    if lax.axis_size("fsdp") != 4:
-        return spread_async(block, "fsdp")
+    if lax.axis_size(S_FSDP) != 4:
+        return spread_async(block, S_FSDP)
     half = block.shape[0] // 2
-    place = lax.axis_index("fsdp")
-    near = lax.ppermute(block, "fsdp", beside(1))
-    side = lax.ppermute(block, "fsdp", beside(2))
-    far_top = lax.ppermute(side[:half], "fsdp", beside(1))
-    far_low = lax.ppermute(near[half:], "fsdp", beside(2))
+    place = lax.axis_index(S_FSDP)
+    near = lax.ppermute(block, S_FSDP, beside(1))
+    side = lax.ppermute(block, S_FSDP, beside(2))
+    far_top = lax.ppermute(side[:half], S_FSDP, beside(1))
+    far_low = lax.ppermute(near[half:], S_FSDP, beside(2))
     whole = jnp.zeros((4, 2, half) + block.shape[1:], block.dtype)
     parts = ((block, place), (near, place ^ 1), (side, place ^ 2))
     for piece, index in parts:
@@ -96,25 +100,25 @@
     def whole(target):
         return jnp.concatenate([make(target, 0), make(target, 1)], axis=0)
 
-    if lax.axis_size("fsdp") != 4:
-        sent = [(route, whole(target).astype(BF)) for route, target, _ in hops("fsdp")]
-        own = whole(lax.axis_index("fsdp"))
+    if lax.axis_size(S_FSDP) != 4:
+        sent = [(route, whole(target).astype(BF)) for route, target, _ in hops(S_FSDP)]
+        own = whole(lax.axis_index(S_FSDP))
         for route, piece in sent:
-            own = own + lax.ppermute(piece, "fsdp", route).astype(F32)
+            own = own + lax.ppermute(piece, S_FSDP, route).astype(F32)
         return own.astype(BF)
-    place = lax.axis_index("fsdp")
-    got_side = lax.ppermute(make(place ^ 3, 0).astype(BF), "fsdp", beside(1))
-    got_near = lax.ppermute(make(place ^ 3, 1).astype(BF), "fsdp", beside(2))
-    near_top = lax.ppermute(make(place ^ 1, 0).astype(BF), "fsdp", beside(1))
-    side_low = lax.ppermute(make(place ^ 2, 1).astype(BF), "fsdp", beside(2))
+    place = lax.axis_index(S_FSDP)
+    got_side = lax.ppermute(make(place ^ 3, 0).astype(BF), S_FSDP, beside(1))
+    got_near = lax.ppermute(make(place ^ 3, 1).astype(BF), S_FSDP, beside(2))
+    near_top = lax.ppermute(make(place ^ 1, 0).astype(BF), S_FSDP, beside(1))
+    side_low = lax.ppermute(make(place ^ 2, 1).astype(BF), S_FSDP, beside(2))
     own_top = make(place, 0).astype(BF)
     own_low = make(place, 1).astype(BF)
     side_top = make(place ^ 2, 0).astype(BF)
     near_low = make(place ^ 1, 1).astype(BF)
     side_top = (side_top.astype(F32) + got_side.astype(F32)).astype(BF)
     near_low = (near_low.astype(F32) + got_near.astype(F32)).astype(BF)
-    side_top = lax.ppermute(side_top, "fsdp", beside(2))
-    near_low = lax.ppermute(near_low, "fsdp", beside(1))
+    side_top = lax.ppermute(side_top, S_FSDP, beside(2))
+    near_low = lax.ppermute(near_low, S_FSDP, beside(1))
     top = own_top.astype(F32) + near_top.astype(F32) + side_top.astype(F32)
     low = own_low.astype(F32) + near_low.astype(F32) + side_low.astype(F32)
     return jnp.concatenate([top, low], axis=0).astype(BF)
@@ -837,10 +841,10 @@
     mlp_out,
     out_grad,
 ):
-    n_f = lax.axis_size("fsdp")
-    n_c = lax.axis_size("context")
-    c_id = lax.axis_index("context")
-    t_id = lax.axis_index("tensor")
+    n_f = lax.axis_size(S_FSDP)
+    n_c = lax.axis_size(S_CONTEXT)
+    c_id = lax.axis_index(S_CONTEXT)
+    t_id = lax.axis_index(S_TENSOR)
     shards = n_f * n_c
     rows = inputs.shape[0]
     group = rows * n_c
@@ -879,12 +883,12 @@
     )
 
     mine = lax.dynamic_slice_in_dim(inputs, t_id * half, half, 0)
-    part = exchange(pack, "context").reshape(n_c * d_loc, p_w)
-    got_in = spread_async(mine, "context")
-    w_all = spread(part, "fsdp").reshape(width, p_w)
+    part = exchange(pack, S_CONTEXT).reshape(n_c * d_loc, p_w)
+    got_in = spread_async(mine, S_CONTEXT)
+    w_all = spread(part, S_FSDP).reshape(width, p_w)
     rows_in = join_pair(got_in, swap_pair(got_in), t_id, 1).reshape(group, width)
-    part_mi = spread_async(mlp_in.reshape(d_loc, 2 * ff), "context")
-    part_mo = spread_async(mlp_out.T, "context")
+    part_mi = spread_async(mlp_in.reshape(d_loc, 2 * ff), S_CONTEXT)
+    part_mo = spread_async(mlp_out.T, S_CONTEXT)
     w_mi = plane_gather(part_mi.reshape(n_c * d_loc, 2 * ff)).reshape(width, 2 * ff)
     w_mo = plane_gather(part_mo.reshape(n_c * d_loc, ff)).reshape(width, ff)
 
@@ -943,7 +947,7 @@
         return (keep.astype(F32) + swap_pair(give).astype(F32)).astype(BF)
 
     summed = pair_add(keep, give).reshape(n_c, half, slab_w)
-    both = jnp.sum(exchange(summed, "context").astype(F32), axis=0)
+    both = jnp.sum(exchange(summed, S_CONTEXT).astype(F32), axis=0)
     squares = jnp.sum(both[:, 2 * width : 2 * width + 4], axis=1, keepdims=True)
     scale_own = lax.rsqrt(squares / plan.total + NORM_EPS)
     mamba_own = both[:, :width]
@@ -977,7 +981,7 @@
     grad_res = top_own + rms_backward(grad_two, normed_two, inv_two, gain_mlp)
     grad_rs_own = jnp.sum(grad_res * mamba_own, axis=1, keepdims=True)
     factor = split(jnp.concatenate([grad_rs_own, scale_own], axis=1), 2)
-    got = spread(jnp.concatenate([grad_res.astype(BF), factor], axis=1), "context")
+    got = spread(jnp.concatenate([grad_res.astype(BF), factor], axis=1), S_CONTEXT)
     got_other = swap_pair(got)
     block = n_c * d_loc
 
@@ -987,7 +991,7 @@
         return dot_tn(cols, mixed)
 
     own = plane_reduce(mlp_block)
-    own = reduce_async(own.reshape(n_c, d_loc, 3 * ff), "context")
+    own = reduce_async(own.reshape(n_c, d_loc, 3 * ff), S_CONTEXT)
     out_mi = own[:, : 2 * ff].reshape(d_loc, 2, ff)
     out_mo = own[:, 2 * ff :].T
 
@@ -1025,16 +1029,16 @@
     mlp_act, residual, keep = lax.optimization_barrier((mlp_act, residual, keep))
     out_own = (residual + pair_sum(dot_nt(mlp_act, w_mo), ())).astype(BF)
     partial = pair_add(keep, give).reshape(n_c, half, width)
-    grad_one = reduce_async(partial, "context")
+    grad_one = reduce_async(partial, S_CONTEXT)
     gain_mix = gain_one[0]
     normed_own, inv_own = rms_forward(in_own)
     grad_in_own = grad_res + rms_backward(grad_one, normed_own, inv_own, gain_mix)
     output = join_pair(out_own, swap_pair(out_own), t_id, 0).reshape(rows, width)
     input_grad = join_pair(grad_in_own, swap_pair(grad_in_own), t_id, 0).reshape(rows, width)
 
-    got = exchange(g_pack.reshape(n_f, block, p_w), "fsdp")
+    got = exchange(g_pack.reshape(n_f, block, p_w), S_FSDP)
     (g_pack,) = call(sum_kernel, plan, [((block, p_w), BF)], [], (), (got,))
-    got = exchange(g_pack.reshape(n_c, d_loc, p_w), "context")
+    got = exchange(g_pack.reshape(n_c, d_loc, p_w), S_CONTEXT)
     out_inner, out_query, out_dt, out_kv, out_mout, out_aout, out_chan, out_heads, tail = call(
         lambda plan, *refs: unpack_kernel(plan, heads_t, q_t, *refs),
         plan,
@@ -1082,7 +1086,7 @@
 
 
 def solution(mesh):
-    both = ("fsdp", "context")
+    both = (S_FSDP, S_CONTEXT)
     rows = P(both, None)
 
     return jax.shard_map(
@@ -1090,38 +1094,38 @@
         mesh=mesh,
         in_specs=(
             rows,
-            P("fsdp", None),
+            P(S_FSDP, None),
             P(None, both),
-            P(both, None, "tensor"),
-            P(both, "tensor"),
+            P(both, None, S_TENSOR),
+            P(both, S_TENSOR),
             rows,
-            P("tensor", both),
+            P(S_TENSOR, both),
             P(None, both),
-            P(None, "tensor"),
-            P(both, "tensor"),
-            P(both, None, "tensor"),
-            P("tensor", both),
-            P("tensor", both),
-            P(both, None, "tensor"),
-            P("tensor", both),
+            P(None, S_TENSOR),
+            P(both, S_TENSOR),
+            P(both, None, S_TENSOR),
+            P(S_TENSOR, both),
+            P(S_TENSOR, both),
+            P(both, None, S_TENSOR),
+            P(S_TENSOR, both),
             rows,
         ),
         out_specs=(
             rows,
             rows,
             P(None, both),
-            P(both, None, "tensor"),
-            P(both, "tensor"),
+            P(both, None, S_TENSOR),
+            P(both, S_TENSOR),
             rows,
-            P("tensor", both),
+            P(S_TENSOR, both),
             P(None, both),
-            P(None, "tensor"),
-            P(both, "tensor"),
-            P(both, None, "tensor"),
-            P("tensor", both),
-            P("tensor", both),
-            P(both, None, "tensor"),
-            P("tensor", both),
+            P(None, S_TENSOR),
+            P(both, S_TENSOR),
+            P(both, None, S_TENSOR),
+            P(S_TENSOR, both),
+            P(S_TENSOR, both),
+            P(both, None, S_TENSOR),
+            P(S_TENSOR, both),
         ),
         check_vma=False,
     )

time: 330 us -> 330 us (level)
  no operation moved by 1% of the time
where the time goes in v2:
time: 330 us; the launch traced here: 328 us
  waiting for transfers between devices  121 us (37%)
  starting transfers between devices  65.2 us (20%)
  local copies, waits for them, and re-layouts  45.1 us (14%)
  Pallas kernels  41.3 us (13%)
  other arithmetic  28.3 us (9%)
  matrix products  25.5 us (8%)
    pallas_call x5, Pallas kernels, call(): pl.pallas_call(lambda *refs: kernel(plan, *refs), out_shape=[jax.ShapeDty...  41.3 us
    ppermute x6, waiting for transfers between devices, reduce_async(): lax.ppermute(lax.dynamic_index_in_dim(blocks, target, 0, False), axis, ro...  32.7 us
    all_to_all x6, waiting for transfers between devices, exchange(): return lax.all_to_all(blocks, axis, 0, 0, tiled=True)  31.4 us
    all_to_all x6, starting transfers between devices, exchange(): return lax.all_to_all(blocks, axis, 0, 0, tiled=True)  24.2 us
    ppermute x2, waiting for transfers between devices, plane_gather(): far_top = lax.ppermute(side[:half], S_FSDP, beside(1))  20.3 us
    ppermute x9, starting transfers between devices, spread_async(): lax.ppermute(block, axis, route)  16.6 us
    dot_general x8, matrix products, dot_tn(): lax.dot_general(left, right, (((0,), (0,)), ((), ())), precision=exact, p...  15.3 us
    dynamic_update_slice x6, local copies, waits for them, and re-layouts, plane_gather(): whole = lax.dynamic_update_slice(whole, piece, (index, 0, 0, 0))  12.3 us
  transfers between devices with their start and end apart: 45, of which 14 were waited for; matrix products, arithmetic and copies ran while one was open for 24% of the time, Pallas kernels for 5%

profile of v2, /device:TPU:0, one launch (start us, length us, event | category | flops | bytes accessed | tf_op | source)
XLA Modules:
  0.0 328.2 jit_solution(9674787500708004218)
XLA Ops:
  1.8 5.1 %collective-permute-start.2 = (bf16[64,1024]{1,0:T(8,128)(2,1)S(1)}, bf16[64,1024]{1,0:T(8,128)(2,1)S(1)}, u32[]{:S(2)}, u32[]{:S(2)}) collective-permute-start(bf16[64,1024]{1,0:T(8,128)(2,1)S(1)} %get-tuple-element.113), channel_id=1, source_target_pairs={{0,6},{2,0},{4,2},{6,4},{1,7},{3,1},{5,3},{7,5},{8,14},{10,8},{12,... | collective-permute-start | bytes 393224 | tf_op jit(solution)/shard_map/ppermute | solution.py:51
  21.5 3.5 %all-to-all-start = ((bf16[4,64,1152]{2,1,0:T(8,128)(2,1)}), bf16[4,64,1152]{2,1,0:T(8,128)(2,1)S(1)}, u32[]{:S(2)}, u32[]{:S(2)}) async-start(bf16[4,64,1152]{2,1,0:T(8,128)(2,1)} %shard_map.271), calls=%async_computation | async-start | bytes 1179648 | tf_op jit(solution)/shard_map/all_to_all | solution.py:34
  29.5 10.2 %all-to-all-done = bf16[4,64,1152]{2,1,0:T(8,128)(2,1)S(1)} async-done(((bf16[4,64,1152]{2,1,0:T(8,128)(2,1)}), bf16[4,64,1152]{2,1,0:T(8,128)(2,1)S(1)}, u32[]{:S(2)}, u32[]{:S(2)}) %all-to-all-start) | async-done | bytes 589856 | tf_op jit(solution)/shard_map/all_to_all | solution.py:34
  41.3 4.6 %all-to-all-start.1 = ((bf16[4,256,1152]{2,1,0:T(8,128)(2,1)}), bf16[4,256,1152]{2,1,0:T(8,128)(2,1)}, u32[]{:S(2)}, u32[]{:S(2)}) async-start(bf16[4,256,1152]{2,1,0:T(8,128)(2,1)} %broadcast_in_dim.35), calls=%async_computation.1 | async-start | bytes 4718592 | tf_op jit(solution)/shard_map/all_to_all | solution.py:34
  47.2 3.6 %collective-permute-start.8 = (bf16[64,2048]{1,0:T(8,128)(2,1)S(1)}, bf16[64,2048]{1,0:T(8,128)(2,1)}, u32[]{:S(2)}, u32[]{:S(2)}) collective-permute-start(bf16[64,2048]{1,0:T(8,128)(2,1)S(1)} %bitcast.181), channel_id=1, source_target_pairs={{0,6},{2,0},{4,2},{6,4},{1,7},{3,1},{5,3},{7,5},{8,14},{10,8},{12,... | collective-permute-start | bytes 786440 | tf_op jit(solution)/shard_map/ppermute | solution.py:51
  62.5 11.7 %all-to-all-done.1 = bf16[4,256,1152]{2,1,0:T(8,128)(2,1)} async-done(((bf16[4,256,1152]{2,1,0:T(8,128)(2,1)}), bf16[4,256,1152]{2,1,0:T(8,128)(2,1)}, u32[]{:S(2)}, u32[]{:S(2)}) %all-to-all-start.1) | async-done | bytes 2359328 | tf_op jit(solution)/shard_map/all_to_all | solution.py:34
  74.2 14.5 %shard_map.272 = (bf16[256,2176]{1,0:T(8,128)(2,1)}, bf16[256,2176]{1,0:T(8,128)(2,1)}, f32[1,1024]{1,0:T(1,128)S(1)}, f32[1,1024]{1,0:T(1,128)S(1)}, f32[8,512]...) custom-call(s32[1,2]{1,0:T(1,128)S(1)} %copy-done.14, ...), custom_call_target="tpu_custom_call" | custom-call | tf_op jit(solution)/shard_map/pallas_call | solution.py:816
  109.0 4.5 %all-to-all-start.2 = ((bf16[4,64,2176]{2,1,0:T(8,128)(2,1)}), bf16[4,64,2176]{2,1,0:T(8,128)(2,1)}, u32[]{:S(2)}, u32[]{:S(2)}) async-start(bf16[4,64,2176]{2,1,0:T(8,128)(2,1)} %bitcast.173), calls=%async_computation.2 | async-start | bytes 2228224 | tf_op jit(solution)/shard_map/all_to_all | solution.py:34
  117.2 15.6 %collective-permute-done.18 = bf16[128,1024]{1,0:T(8,128)(2,1)S(1)} collective-permute-done((bf16[128,1024]{1,0:T(8,128)(2,1)}, bf16[128,1024]{1,0:T(8,128)(2,1)S(1)}, u32[]{:S(2)}, u32[]{:S(2)}) %collective-permute-start.18) | collective-permute-done | bytes 262176 | tf_op jit(solution)/shard_map/ppermute | solution.py:87
  143.1 4.7 %collective-permute-done.11 = bf16[128,2048]{1,0:T(8,128)(2,1)S(1)} collective-permute-done((bf16[128,2048]{1,0:T(8,128)(2,1)S(1)}, bf16[128,2048]{1,0:T(8,128)(2,1)S(1)}, u32[]{:S(2)}, u32[]{:S(2)}) %collective-permute-start.11) | collective-permute-done | bytes 524320 | tf_op jit(solution)/shard_map/ppermute | solution.py:87
  156.9 3.9 %fusion.90 = f32[2,64,1024]{2,1,0:T(8,128)S(1)} fusion(bf16[2,64,2048]{2,1,0:T(8,128)(2,1)S(1)} %bitcast.179, bf16[1024,2048,1]{1,0,2:T(8,128)(2,1)} %bitcast.44), kind=kOutput, calls=%fused_computation.208 | convolution fusion | flops 536870912 | bytes 5242880 | tf_op jit(solution)/shard_map/dot_general | solution.py:152
  169.7 4.4 %all-to-all-start.3 = ((bf16[4,64,1152]{2,1,0:T(8,128)(2,1)}), bf16[4,64,1152]{2,1,0:T(8,128)(2,1)S(1)}, u32[]{:S(2)}, u32[]{:S(2)}) async-start(bf16[4,64,1152]{2,1,0:T(8,128)(2,1)} %broadcast_in_dim.73), calls=%async_computation.3 | async-start | bytes 1179648 | tf_op jit(solution)/shard_map/all_to_all | solution.py:34
  174.1 10.9 %collective-permute-done.31 = bf16[128,3072]{1,0:T(8,128)(2,1)} collective-permute-done((bf16[128,3072]{1,0:T(8,128)(2,1)}, bf16[128,3072]{1,0:T(8,128)(2,1)}, u32[]{:S(2)}, u32[]{:S(2)}) %collective-permute-start.31) | collective-permute-done | bytes 786464 | tf_op jit(solution)/shard_map/ppermute | solution.py:110
  198.0 3.8 %collective-permute-done.30 = bf16[128,3072]{1,0:T(8,128)(2,1)} collective-permute-done((bf16[128,3072]{1,0:T(8,128)(2,1)}, bf16[128,3072]{1,0:T(8,128)(2,1)}, u32[]{:S(2)}, u32[]{:S(2)}) %collective-permute-start.30) | collective-permute-done | bytes 786464 | tf_op jit(solution)/shard_map/ppermute | solution.py:112
  201.8 6.7 %collective-permute-done.32 = bf16[128,3072]{1,0:T(8,128)(2,1)} collective-permute-done((bf16[128,3072]{1,0:T(8,128)(2,1)}, bf16[128,3072]{1,0:T(8,128)(2,1)}, u32[]{:S(2)}, u32[]{:S(2)}) %collective-permute-start.32) | collective-permute-done | bytes 786464 | tf_op jit(solution)/shard_map/ppermute | solution.py:120
  210.6 12.2 %collective-permute-done.35 = bf16[128,3072]{1,0:T(8,128)(2,1)} collective-permute-done((bf16[128,3072]{1,0:T(8,128)(2,1)}, bf16[128,3072]{1,0:T(8,128)(2,1)}, u32[]{:S(2)}, u32[]{:S(2)}) %collective-permute-start.35) | collective-permute-done | bytes 786464 | tf_op jit(solution)/shard_map/ppermute | solution.py:113
  226.1 23.2 %shard_map.273 = (bf16[256,1024]{1,0:T(8,128)(2,1)S(1)}, bf16[256,1024]{1,0:T(8,128)(2,1)S(1)}, bf16[1024,1152]{1,0:T(8,128)(2,1)}) custom-call(s32[1,2]{1,0:T(1,128)S(1)} %copy-done.14, f32[3,3]{1,0:T(4,128)S(1)} %constant_dynamic-slice_fusion.refs_1_, s32[1]{0:T(128)} %bitcast.refs_2_, bf16[512,1024]{1,0:T(8,128)(2,1)S(1)} %bitcast.157, ...), custom_call_target="tpu_custom_call" | custom-call | tf_op jit(solution)/shard_map/pallas_call | solution.py:816
  250.9 3.8 %all-to-all-start.4 = ((bf16[4,256,1152]{2,1,0:T(8,128)(2,1)}), bf16[4,256,1152]{2,1,0:T(8,128)(2,1)S(1)}, u32[]{:S(2)}, u32[]{:S(2)}) async-start(bf16[4,256,1152]{2,1,0:T(8,128)(2,1)} %bitcast.177), calls=%async_computation.4 | async-start | bytes 4718592 | tf_op jit(solution)/shard_map/all_to_all | solution.py:34
  259.5 3.3 collective-permute-start.38
  263.2 3.8 %collective-permute-start.27 = (bf16[64,1024]{1,0:T(8,128)(2,1)S(1)}, bf16[64,1024]{1,0:T(8,128)(2,1)S(1)}, u32[]{:S(2)}, u32[]{:S(2)}) collective-permute-start(bf16[64,1024]{1,0:T(8,128)(2,1)S(1)} %get-tuple-element.133), channel_id=1, source_target_pairs={{0,6},{2,0},{4,2},{6,4},{1,7},{3,1},{5,3},{7,5},{8,14},{10,8},{12,... | collective-permute-start | bytes 393224 | tf_op jit(solution)/shard_map/ppermute | solution.py:67
  267.8 16.4 %collective-permute-done.25 = bf16[64,1024]{1,0:T(8,128)(2,1)S(1)} collective-permute-done((bf16[64,1024]{1,0:T(8,128)(2,1)S(1)}, bf16[64,1024]{1,0:T(8,128)(2,1)S(1)}, u32[]{:S(2)}, u32[]{:S(2)}) %collective-permute-start.25) | collective-permute-done | bytes 131104 | tf_op jit(solution)/shard_map/ppermute | solution.py:67
  286.8 13.4 %collective-permute-done.26 = bf16[64,1024]{1,0:T(8,128)(2,1)S(1)} collective-permute-done((bf16[64,1024]{1,0:T(8,128)(2,1)S(1)}, bf16[64,1024]{1,0:T(8,128)(2,1)S(1)}, u32[]{:S(2)}, u32[]{:S(2)}) %collective-permute-start.26) | collective-permute-done | bytes 131104 | tf_op jit(solution)/shard_map/ppermute | solution.py:67
  302.2 3.5 %all-to-all-start.5 = ((bf16[4,64,1152]{2,1,0:T(8,128)(2,1)}), bf16[4,64,1152]{2,1,0:T(8,128)(2,1)S(1)}, u32[]{:S(2)}, u32[]{:S(2)}) async-start(bf16[4,64,1152]{2,1,0:T(8,128)(2,1)} %bitcast.67), calls=%async_computation.5 | async-start | bytes 1179648 | tf_op jit(solution)/shard_map/all_to_all | solution.py:34
  313.0 9.4 %all-to-all-done.5.refs_0_ = bf16[4,64,1152]{2,1,0:T(8,128)(2,1)S(1)} async-done(((bf16[4,64,1152]{2,1,0:T(8,128)(2,1)}), bf16[4,64,1152]{2,1,0:T(8,128)(2,1)S(1)}, u32[]{:S(2)}, u32[]{:S(2)}) %all-to-all-start.5) | async-done | bytes 589856 | tf_op jit(solution)/shard_map/all_to_all | solution.py:34
  (283 shorter events, 129.8 us)
Async XLA Ops:
  1.8 45.1 %collective-permute-start.2 = (bf16[64,1024]{1,0:T(8,128)(2,1)S(1)}, bf16[64,1024]{1,0:T(8,128)(2,1)S(1)}, u32[]{:S(2)}, u32[]{:S(2)}) collective-permute-start(bf16[64,1024]{1,0:T(8,128)(2,1)S(1)} %get-tuple-element.113), channel_id=1, source_target_pairs={{0,6},{2,0},{4,2},{6,4},{1,7},{3,1},{5,3},{7,5},{8,14},{10,8},{12,... | collective-permute-start | bytes 393224 | tf_op jit(solution)/shard_map/ppermute | solution.py:51
  6.9 40.3 %collective-permute-start.1 = (bf16[64,1024]{1,0:T(8,128)(2,1)S(1)}, bf16[64,1024]{1,0:T(8,128)(2,1)}, u32[]{:S(2)}, u32[]{:S(2)}) collective-permute-start(bf16[64,1024]{1,0:T(8,128)(2,1)S(1)} %get-tuple-element.113), channel_id=1, source_target_pairs={{0,4},{2,6},{4,0},{6,2},{1,5},{3,7},{5,1},{7,3},{8,12},{10,14},{12... | collective-permute-start | bytes 393224 | tf_op jit(solution)/shard_map/ppermute | solution.py:51
  6.9 43.8 %collective-permute-start = (bf16[64,1024]{1,0:T(8,128)(2,1)S(1)}, bf16[64,1024]{1,0:T(8,128)(2,1)}, u32[]{:S(2)}, u32[]{:S(2)}) collective-permute-start(bf16[64,1024]{1,0:T(8,128)(2,1)S(1)} %get-tuple-element.113), channel_id=1, source_target_pairs={{0,2},{2,4},{4,6},{6,0},{1,3},{3,5},{5,7},{7,1},{8,10},{10,12},{12... | collective-permute-start | bytes 393224 | tf_op jit(solution)/shard_map/ppermute | solution.py:51
  7.9 47.5 %collective-permute-start.14 = (bf16[64,1024]{1,0:T(8,128)(2,1)}, bf16[64,1024]{1,0:T(8,128)(2,1)}, u32[]{:S(2)}, u32[]{:S(2)}) collective-permute-start(bf16[64,1024]{1,0:T(8,128)(2,1)} %bitcast.199), channel_id=1, source_target_pairs={{0,4},{2,6},{4,0},{6,2},{1,5},{3,7},{5,1},{7,3},{8,12},{10,14},{12... | collective-permute-start | bytes 393224 | tf_op jit(solution)/shard_map/ppermute | solution.py:51
  9.8 45.7 %collective-permute-start.15 = (bf16[64,1024]{1,0:T(8,128)(2,1)}, bf16[64,1024]{1,0:T(8,128)(2,1)}, u32[]{:S(2)}, u32[]{:S(2)}) collective-permute-start(bf16[64,1024]{1,0:T(8,128)(2,1)} %bitcast.200), channel_id=1, source_target_pairs={{0,6},{2,0},{4,2},{6,4},{1,7},{3,1},{5,3},{7,5},{8,14},{10,8},{12,... | collective-permute-start | bytes 393224 | tf_op jit(solution)/shard_map/ppermute | solution.py:51
  41.3 32.9 %all-to-all-start.1 = ((bf16[4,256,1152]{2,1,0:T(8,128)(2,1)}), bf16[4,256,1152]{2,1,0:T(8,128)(2,1)}, u32[]{:S(2)}, u32[]{:S(2)}) async-start(bf16[4,256,1152]{2,1,0:T(8,128)(2,1)} %broadcast_in_dim.35), calls=%async_computation.1 | async-start | bytes 4718592 | tf_op jit(solution)/shard_map/all_to_all | solution.py:34
  47.2 43.4 %collective-permute-start.8 = (bf16[64,2048]{1,0:T(8,128)(2,1)S(1)}, bf16[64,2048]{1,0:T(8,128)(2,1)}, u32[]{:S(2)}, u32[]{:S(2)}) collective-permute-start(bf16[64,2048]{1,0:T(8,128)(2,1)S(1)} %bitcast.181), channel_id=1, source_target_pairs={{0,6},{2,0},{4,2},{6,4},{1,7},{3,1},{5,3},{7,5},{8,14},{10,8},{12,... | collective-permute-start | bytes 786440 | tf_op jit(solution)/shard_map/ppermute | solution.py:51
  55.4 35.8 %collective-permute-start.7 = (bf16[64,2048]{1,0:T(8,128)(2,1)S(1)}, bf16[64,2048]{1,0:T(8,128)(2,1)S(1)}, u32[]{:S(2)}, u32[]{:S(2)}) collective-permute-start(bf16[64,2048]{1,0:T(8,128)(2,1)S(1)} %bitcast.182), channel_id=1, source_target_pairs={{0,4},{2,6},{4,0},{6,2},{1,5},{3,7},{5,1},{7,3},{8,12},{10,14},{12... | collective-permute-start | bytes 786440 | tf_op jit(solution)/shard_map/ppermute | solution.py:51
  55.5 35.7 %collective-permute-start.6 = (bf16[64,2048]{1,0:T(8,128)(2,1)S(1)}, bf16[64,2048]{1,0:T(8,128)(2,1)}, u32[]{:S(2)}, u32[]{:S(2)}) collective-permute-start(bf16[64,2048]{1,0:T(8,128)(2,1)S(1)} %bitcast.183), channel_id=1, source_target_pairs={{0,2},{2,4},{4,6},{6,0},{1,3},{3,5},{5,7},{7,1},{8,10},{10,12},{12... | collective-permute-start | bytes 786440 | tf_op jit(solution)/shard_map/ppermute | solution.py:51
  59.2 41.3 %collective-permute-start.17 = (bf16[256,1024]{1,0:T(8,128)(2,1)}, bf16[256,1024]{1,0:T(8,128)(2,1)}, u32[]{:S(2)}, u32[]{:S(2)}) collective-permute-start(bf16[256,1024]{1,0:T(8,128)(2,1)} %bitcast.36), channel_id=1, source_target_pairs={{0,16},{8,24},{16,0},{24,8},{1,17},{9,25},{17,1},{25,9},{2,18},{10... | collective-permute-start | bytes 1572872 | tf_op jit(solution)/shard_map/ppermute | solution.py:86
  93.5 40.0 %collective-permute-start.10 = (bf16[256,2048]{1,0:T(8,128)(2,1)}, bf16[256,2048]{1,0:T(8,128)(2,1)}, u32[]{:S(2)}, u32[]{:S(2)}) collective-permute-start(bf16[256,2048]{1,0:T(8,128)(2,1)} %bitcast.24), channel_id=1, source_target_pairs={{0,16},{8,24},{16,0},{24,8},{1,17},{9,25},{17,1},{25,9},{2,18},{10... | collective-permute-start | bytes 3145736 | tf_op jit(solution)/shard_map/ppermute | solution.py:86
  94.1 41.9 %collective-permute-start.9 = (bf16[256,2048]{1,0:T(8,128)(2,1)}, bf16[256,2048]{1,0:T(8,128)(2,1)}, u32[]{:S(2)}, u32[]{:S(2)}) collective-permute-start(bf16[256,2048]{1,0:T(8,128)(2,1)} %bitcast.24), channel_id=1, source_target_pairs={{0,8},{8,0},{16,24},{24,16},{1,9},{9,1},{17,25},{25,17},{2,10},{10... | collective-permute-start | bytes 3145736 | tf_op jit(solution)/shard_map/ppermute | solution.py:85
  102.1 30.7 %collective-permute-start.18 = (bf16[128,1024]{1,0:T(8,128)(2,1)}, bf16[128,1024]{1,0:T(8,128)(2,1)S(1)}, u32[]{:S(2)}, u32[]{:S(2)}) collective-permute-start(bf16[128,1024]{1,0:T(8,128)(2,1)} %slice.65), channel_id=1, source_target_pairs={{0,8},{8,0},{16,24},{24,16},{1,9},{9,1},{17,25},{25,17},{2,10},{10... | collective-permute-start | bytes 786440 | tf_op jit(solution)/shard_map/ppermute | solution.py:87
  107.1 28.2 %collective-permute-start.19 = (bf16[128,1024]{1,0:T(8,128)(2,1)}, bf16[128,1024]{1,0:T(8,128)(2,1)S(1)}, u32[]{:S(2)}, u32[]{:S(2)}) collective-permute-start(bf16[128,1024]{1,0:T(8,128)(2,1)} %slice.66), channel_id=1, source_target_pairs={{0,16},{8,24},{16,0},{24,8},{1,17},{9,25},{17,1},{25,9},{2,18},{10... | collective-permute-start | bytes 786440 | tf_op jit(solution)/shard_map/ppermute | solution.py:88
  109.0 39.7 %all-to-all-start.2 = ((bf16[4,64,2176]{2,1,0:T(8,128)(2,1)}), bf16[4,64,2176]{2,1,0:T(8,128)(2,1)}, u32[]{:S(2)}, u32[]{:S(2)}) async-start(bf16[4,64,2176]{2,1,0:T(8,128)(2,1)} %bitcast.173), calls=%async_computation.2 | async-start | bytes 2228224 | tf_op jit(solution)/shard_map/all_to_all | solution.py:34
  163.7 28.8 %collective-permute-start.33 = (bf16[128,3072]{1,0:T(8,128)(2,1)}, bf16[128,3072]{1,0:T(8,128)(2,1)}, u32[]{:S(2)}, u32[]{:S(2)}) collective-permute-start(bf16[128,3072]{1,0:T(8,128)(2,1)} %convolution_convert_fusion.1), channel_id=1, source_target_pairs={{0,16},{8,24},{16,0},{24,8},{1,17},{9,25},{17,1},{25,9},{2,18},{10... | collective-permute-start | bytes 2359304 | tf_op jit(solution)/shard_map/ppermute | solution.py:111
  166.9 34.9 %collective-permute-start.30 = (bf16[128,3072]{1,0:T(8,128)(2,1)}, bf16[128,3072]{1,0:T(8,128)(2,1)}, u32[]{:S(2)}, u32[]{:S(2)}) collective-permute-start(bf16[128,3072]{1,0:T(8,128)(2,1)} %convolution_convert_fusion.6), channel_id=1, source_target_pairs={{0,8},{8,0},{16,24},{24,16},{1,9},{9,1},{17,25},{25,17},{2,10},{10... | collective-permute-start | bytes 2359304 | tf_op jit(solution)/shard_map/ppermute | solution.py:112
  169.7 28.2 %all-to-all-start.3 = ((bf16[4,64,1152]{2,1,0:T(8,128)(2,1)}), bf16[4,64,1152]{2,1,0:T(8,128)(2,1)S(1)}, u32[]{:S(2)}, u32[]{:S(2)}) async-start(bf16[4,64,1152]{2,1,0:T(8,128)(2,1)} %broadcast_in_dim.73), calls=%async_computation.3 | async-start | bytes 1179648 | tf_op jit(solution)/shard_map/all_to_all | solution.py:34
  191.9 30.9 %collective-permute-start.35 = (bf16[128,3072]{1,0:T(8,128)(2,1)}, bf16[128,3072]{1,0:T(8,128)(2,1)}, u32[]{:S(2)}, u32[]{:S(2)}) collective-permute-start(bf16[128,3072]{1,0:T(8,128)(2,1)} %convolution_convert_fusion), channel_id=1, source_target_pairs={{0,16},{8,24},{16,0},{24,8},{1,17},{9,25},{17,1},{25,9},{2,18},{10... | collective-permute-start | bytes 2359304 | tf_op jit(solution)/shard_map/ppermute | solution.py:113
  197.9 28.2 %collective-permute-start.21 = (bf16[4,64,1152]{2,1,0:T(8,128)(2,1)S(1)}, bf16[4,64,1152]{2,1,0:T(8,128)(2,1)S(1)}, u32[]{:S(2)}, u32[]{:S(2)}) collective-permute-start(bf16[4,64,1152]{2,1,0:T(8,128)(2,1)S(1)} %all-to-all-done.3.refs_13_), channel_id=1, source_target_pairs={{0,1},{1,0},{2,3},{3,2},{4,5},{5,4},{6,7},{7,6},{8,9},{9,8},{10,11... | collective-permute-start | bytes 1769480 | tf_op jit(solution)/shard_map/ppermute | solution.py:24
  250.9 49.8 %all-to-all-start.4 = ((bf16[4,256,1152]{2,1,0:T(8,128)(2,1)}), bf16[4,256,1152]{2,1,0:T(8,128)(2,1)S(1)}, u32[]{:S(2)}, u32[]{:S(2)}) async-start(bf16[4,256,1152]{2,1,0:T(8,128)(2,1)} %bitcast.177), calls=%async_computation.4 | async-start | bytes 4718592 | tf_op jit(solution)/shard_map/all_to_all | solution.py:34
  258.9 46.7 %collective-permute-start.36 = (bf16[64,3072]{1,0:T(8,128)(2,1)}, bf16[64,3072]{1,0:T(8,128)(2,1)S(1)}, u32[]{:S(2)}, u32[]{:S(2)}) collective-permute-start(bf16[64,3072]{1,0:T(8,128)(2,1)} %get-tuple-element.118), channel_id=1, source_target_pairs={{0,2},{2,4},{4,6},{6,0},{1,3},{3,5},{5,7},{7,1},{8,10},{10,12},{12... | collective-permute-start | bytes 1179656 | tf_op jit(solution)/shard_map/ppermute | solution.py:67
  259.5 46.2 %collective-permute-start.38 = (bf16[64,3072]{1,0:T(8,128)(2,1)}, bf16[64,3072]{1,0:T(8,128)(2,1)}, u32[]{:S(2)}, u32[]{:S(2)}) collective-permute-start(bf16[64,3072]{1,0:T(8,128)(2,1)} %get-tuple-element.119), channel_id=1, source_target_pairs={{0,6},{2,0},{4,2},{6,4},{1,7},{3,1},{5,3},{7,5},{8,14},{10,8},{12,... | collective-permute-start | bytes 1179656 | tf_op jit(solution)/shard_map/ppermute | solution.py:67
  267.0 33.2 %collective-permute-start.26 = (bf16[64,1024]{1,0:T(8,128)(2,1)S(1)}, bf16[64,1024]{1,0:T(8,128)(2,1)S(1)}, u32[]{:S(2)}, u32[]{:S(2)}) collective-permute-start(bf16[64,1024]{1,0:T(8,128)(2,1)S(1)} %get-tuple-element.134), channel_id=1, source_target_pairs={{0,4},{2,6},{4,0},{6,2},{1,5},{3,7},{5,1},{7,3},{8,12},{10,14},{12... | collective-permute-start | bytes 393224 | tf_op jit(solution)/shard_map/ppermute | solution.py:67
  (71 other events, 915.2 us)
